TPU v7x, 512 devices: a whole 4x4x16 slice. The times are simulated.
512 devices in a mesh: wide: 64 (over y_lo, z, core), narrow: 8 (over x, y_hi).
Axes of the slice: x: 4, y: 4 (y_hi: 2, y_lo: 2; y = y_hi * 2 + y_lo), z: 16, core: 2. Of those that a mesh axis runs over, the one named last changes fastest.
Arguments:
- cell_rows: bfloat16 [32768, 2048], P('wide', 'narrow'), may hold values from -3 to 3
- attn_gain: float32 [2048], replicated, may hold values from 0.1 to 1.9
- ffn_gain: float32 [2048], replicated, may hold values from 0.1 to 1.9
- panels: bfloat16 [64, 2048, 4096], P('wide', None, 'narrow'), may hold values from -0.125 to 0.125
- panel_slot: int32 [64], replicated, may hold values from 0 to 63, each once
- layout: int32 [256, 3], P('wide'), may hold values from 0 to 31, as said below
Outputs:
- encoded: bfloat16 [32768, 2048], P('wide', 'narrow')
Inputs may be any that keep to these rules, and one draw needn't show every extreme that they name: `panel_slot`: the first three entries name the indices of wide that hold this layer's attention panel, feed-forward input panel and feed-forward output panel; all entries differ. `layout`: row b lists the position p(b) of block b itself first, then two other positions of the same netlist at most 2 away; the three differ. One of the two lies before p(b) and one after it, except for the first two and last two positions of a netlist.
All inputs are finite; a program needn't handle non-finite values.
Results may differ from a plain program's by a relative error of at most 0.018.
Values may be sent and summed in bfloat16 or wider, within the bound.
A program may use at most 64 MiB of HBM per device.

v0:
```python
import jax
import jax.numpy as jnp
from jax import lax
from jax.sharding import PartitionSpec as P

HD = 128
BLK = 128
NET_BLOCKS = 32


epsilon = 1e-05


def spread(block, axis, source):
    block = jnp.where(lax.axis_index(axis) == source, block, jnp.zeros_like(block))
    return lax.psum(block, axis)


def extended(shard, sides, width):
    for axis, dim in sides:
        size, length = (lax.axis_size(axis), shard.shape[dim])
        up = [(i, (i + 1) % size) for i in range(size - 1)]
        down = [(j, i) for i, j in up]
        last = lax.slice_in_dim(shard, length - width, length, axis=dim)
        first = lax.slice_in_dim(shard, 0, width, axis=dim)
        before = lax.ppermute(last, axis, up)
        after = lax.ppermute(first, axis, down)
        shard = jnp.concatenate([before, shard, after], axis=dim)
    return shard


def rms_scale(values, gain):
    mean_square = jnp.mean(values * values, axis=-1, keepdims=True)
    return values * lax.rsqrt(mean_square + epsilon) * gain


def block_mask(layout, query_index):
    wanted = query_index[:, None] + jnp.arange(5, dtype=jnp.int32)[None, :] - 2
    return jnp.any(layout[:, :, None] == wanted[:, None, :], axis=1)


def on_device(cell_rows, attn_gain, ffn_gain, panels, panel_slot, layout):
    attn_panel = spread(panels[0], "wide", panel_slot[0])
    row_count = cell_rows.shape[0]
    block_count = row_count // BLK
    cell_full = lax.all_gather(cell_rows, "narrow", axis=1, tiled=True)
    normed = rms_scale(cell_full.astype(jnp.float32), attn_gain).astype(jnp.bfloat16)
    model_width = attn_panel.shape[0]
    head_count = attn_panel.shape[1] // (4 * HD)
    attn_table = attn_panel.reshape(model_width, head_count, 4, HD)
    projected = jnp.einsum(
        "td,dhjc->thjc", normed, attn_table[:, :, :3, :], preferred_element_type=jnp.float32
    ).astype(jnp.bfloat16)
    key_values = projected[:, :, 1:, :].reshape(row_count, head_count * 2 * HD)
    key_window = extended(key_values, (("wide", 0),), 2 * BLK)
    pair_blocks = key_window.reshape(block_count + 4, BLK, head_count, 2, HD)
    stacked = jnp.stack([pair_blocks[offset : offset + block_count] for offset in range(5)], axis=1)
    query_index = (
        lax.axis_index("wide") * block_count
        + jnp.arange(block_count, dtype=jnp.int32)
        + block_count // 2
    ) % NET_BLOCKS
    allowed = block_mask(layout, query_index)
    queries = projected[:, :, 0, :].reshape(block_count, BLK, head_count, HD)
    scores = jnp.einsum(
        "bqhc,bokhc->bhqok", queries, stacked[:, :, :, :, 0, :], preferred_element_type=jnp.float32
    ) * HD ** (-0.5)
    lifted = jnp.where(allowed[:, None, None, :, None], jnp.exp(scores), jnp.float32(0.0))
    weights = (lifted / jnp.sum(lifted, axis=(3, 4), keepdims=True)).astype(jnp.bfloat16)
    head_out = jnp.einsum(
        "bhqok,bokhc->bqhc", weights, stacked[:, :, :, :, 1, :], preferred_element_type=jnp.float32
    ).astype(jnp.bfloat16)
    head_out = head_out.reshape(row_count, head_count * HD)
    out_rows = attn_table[:, :, 3, :].reshape(model_width, head_count * HD)
    partial_value = lax.dot_general(
        head_out, out_rows, (((1,), (1,)), ((), ())), preferred_element_type=jnp.float32
    )
    attn_part = lax.psum_scatter(
        partial_value.astype(jnp.bfloat16), "narrow", scatter_dimension=1, tiled=True
    ).astype(jnp.float32)
    stream = (cell_rows.astype(jnp.float32) + attn_part).astype(jnp.bfloat16)
    stream_full = lax.all_gather(stream, "narrow", axis=1, tiled=True)
    up_panel = spread(panels[0], "wide", panel_slot[1])
    down_panel = spread(panels[0], "wide", panel_slot[2])
    normed_ffn = rms_scale(stream_full.astype(jnp.float32), ffn_gain).astype(jnp.bfloat16)
    hidden = jax.nn.gelu(
        jnp.dot(normed_ffn, up_panel, preferred_element_type=jnp.float32), approximate=False
    ).astype(jnp.bfloat16)
    ffn_part = lax.dot_general(
        hidden, down_panel, (((1,), (1,)), ((), ())), preferred_element_type=jnp.float32
    )
    mixed_units = lax.psum_scatter(
        ffn_part.astype(jnp.bfloat16), "narrow", scatter_dimension=1, tiled=True
    ).astype(jnp.float32)
    return (stream.astype(jnp.float32) + mixed_units).astype(jnp.bfloat16)


def solution(mesh):
    return jax.shard_map(
        on_device,
        mesh=mesh,
        in_specs=(P("wide", "narrow"), P(), P(), P("wide", None, "narrow"), P(), P("wide", None)),
        out_specs=P("wide", "narrow"),
        check_vma=False,
    )
```

profile of v0, /device:TPU:1, one launch (start us, length us, event | category | flops | bytes accessed | tf_op | source)
XLA Modules:
  0.0 769.1 jit_solution(15220941853354655202)
XLA Ops:
  7.4 0.0 all-gather.3.cloned.1.call-start
  7.4 0.7 all-gather.3.cloned.1.call-update
  8.1 0.0 all-reduce.3.cloned.1.call-start
  8.1 1.4 fusion.95
  11.5 4.0 broadcast_select_fusion
  15.4 2.4 copy.23
  17.8 0.0 all-reduce.3.cloned.1.call-update
  17.9 0.0 reduce-scatter.3.cloned.1.call-start
  17.9 71.7 %all-gather.3.cloned.1.call-done = bf16[512,2048]{1,0:T(8,128)(2,1)} async-done(((bf16[512,256]{1,0:T(8,128)(2,1)}), bf16[512,2048]{1,0:T(8,128)(2,1)}) %all-gather.3.cloned.1.call-update) | async-done | bytes 2097168 | tf_op jit(solution)/shard_map/all_gather | solution.py:46
  89.7 2.1 fusion
  91.8 0.0 copy-start.1
  91.8 0.0 copy-start.6
  91.8 386.0 %all-reduce.3.cloned.1.call-done = (bf16[2048,512]{1,0:T(8,128)(2,1)}, bf16[2048,512]{1,0:T(8,128)(2,1)}, bf16[2048,1,4,128]{0,3,2,1:T(8,128)(2,1)}) async-done(((bf16[2048,512]{1,0:T(8,128)(2,1)}, bf16[2048,512]{1,0:T(8,128)(2,1)}, bf16[2048,1,4,128]{0,3,2,1:T(8,128)(2,1)}), (bf16[2048,512]{1,0:T(8,128)(2,1)}, bf16[2048,512]{1,0:T(8,128)(2,1)}, ...) | async-done | bytes 6291472 | tf_op jit(solution)/shard_map/psum | solution.py:16
  477.8 1.5 slice.80
  479.3 0.0 copy-done.1
  479.3 0.0 copy-done.6
  479.3 1.1 fusion.8
  480.4 0.0 copy-start.5
  480.4 0.1 convert_bitcast_fusion
  480.5 0.1 copy.24
  480.6 2.9 collective-permute-start
  483.5 0.1 copy.26
  483.6 1.9 collective-permute-start.1
  485.6 0.1 add_add_fusion
  485.6 0.0 copy-done.5
  485.7 0.1 copy.33
  485.7 0.1 compare_reduce_fusion
  485.9 0.2 copy.39
  486.0 0.1 copy.25
  486.2 0.1 copy.40
  486.3 0.0 collective-permute-done
  486.3 3.6 collective-permute-done.1
  489.9 0.1 pad_maximum_fusion
  490.0 0.1 stack.18
  490.1 0.7 copy_dynamic-update-slice_fusion.3
  490.8 0.1 stack.19
  490.9 0.1 stack.21
  491.0 0.1 stack.22
  491.0 0.7 copy_dynamic-update-slice_fusion.2
  491.8 0.8 constant_dynamic-update-slice_fusion
  492.5 0.7 copy_dynamic-update-slice_fusion.1
  493.3 0.7 copy_dynamic-update-slice_fusion
  494.0 1.6 fusion.96
  495.6 0.0 copy-done.4
  495.6 0.4 fusion.16
  496.0 0.0 copy-start.3
  496.1 3.1 convolution_convert_fusion
  499.2 0.0 reduce-scatter.3.cloned.1.call-update
  499.2 0.0 copy-start.7
  499.2 0.0 all-gather.5.cloned.1.call-start
  499.3 85.2 %reduce-scatter.3.cloned.1.call-done = bf16[512,256]{1,0:T(8,128)(2,1)} async-done(((bf16[512,2048]{1,0:T(8,128)(2,1)}), bf16[512,256]{1,0:T(8,128)(2,1)}) %reduce-scatter.3.cloned.1.call-update) | async-done | bytes 262160 | tf_op jit(solution)/shard_map/reduce_scatter | solution.py:78
  584.5 0.0 copy-done.3
  584.5 1.7 add_convert_fusion.1
  586.2 0.0 all-gather.5.cloned.1.call-update
  586.2 0.0 reduce-scatter.5.cloned.1.call-start
  586.3 72.4 %all-gather.5.cloned.1.call-done = bf16[512,2048]{1,0:T(8,128)(2,1)} async-done(((bf16[512,256]{1,0:T(8,128)(2,1)}), bf16[512,2048]{1,0:T(8,128)(2,1)}) %all-gather.5.cloned.1.call-update) | async-done | bytes 2097168 | tf_op jit(solution)/shard_map/all_gather | solution.py:82
  658.7 2.2 fusion.3
  660.9 0.0 copy-done.7
  660.9 0.0 copy-done.2
  661.0 8.1 %convolution_convert_fusion.1 = bf16[512,2048]{1,0:T(8,128)(2,1)} fusion(bf16[2048,512]{1,0:T(8,128)(2,1)} %get-tuple-element.5, bf16[2048,512]{1,0:T(8,128)(2,1)} %get-tuple-element.6, bf16[512,2048]{1,0:T(8,128)(2,1)S(1)} %copy-done.2, f32[2048]{0:T(1024)S(1)} %copy-done.7, f32[512]{0:T(512)S(1)} %add_rsqrt_fusion), kind=kOutput, calls=%fused_computation.11 | convolution fusion | flops 2169765888 | bytes 8398848 | tf_op jit(solution)/shard_map/dot_general | solution.py:89
  669.0 0.0 reduce-scatter.5.cloned.1.call-update
  669.1 91.2 %reduce-scatter.5.cloned.1.call-done = bf16[512,256]{1,0:T(8,128)(2,1)} async-done(((bf16[512,2048]{1,0:T(8,128)(2,1)}), bf16[512,256]{1,0:T(8,128)(2,1)}) %reduce-scatter.5.cloned.1.call-update) | async-done | bytes 262160 | tf_op jit(solution)/shard_map/reduce_scatter | solution.py:92
  760.2 0.0 copy-done
  760.3 1.7 add_convert_fusion
  (9 shorter events, 0.1 us)
Async XLA Ops:
  7.4 82.3 %all-gather.3.cloned.1.call-start = ((), (), s32[]{:S(2)}) async-start(), calls=%async_computation.2 | async-start | bytes 2359296 | tf_op jit(solution)/shard_map/all_gather | solution.py:46
  8.1 469.7 %all-reduce.3.cloned.1.call-start = ((), (), s32[]{:S(2)}) async-start(), calls=%async_computation.6 | async-start | bytes 12582912 | tf_op jit(solution)/shard_map/psum | solution.py:16
  17.9 566.6 %reduce-scatter.3.cloned.1.call-start = ((), (), s32[]{:S(2)}) async-start(), calls=%async_computation.3 | async-start | bytes 2359296 | tf_op jit(solution)/shard_map/reduce_scatter | solution.py:78
  91.8 387.5 %copy-start.1 = (bf16[512,2048]{1,0:T(8,128)(2,1)S(1)}, bf16[512,2048]{1,0:T(8,128)(2,1)}, u32[]{:S(2)}) copy-start(bf16[512,2048]{1,0:T(8,128)(2,1)} %all-gather.3.cloned.1.call-done) | copy-start | bytes 6291460
  91.8 387.5 %copy-start.6 = (f32[2048]{0:T(1024)S(1)}, f32[2048]{0:T(1024)}, u32[]{:S(2)}) copy-start(f32[2048]{0:T(1024)} %param.7) | copy-start | bytes 24580
  480.4 5.2 copy-start.5
  480.6 5.7 collective-permute-start
  483.6 6.3 collective-permute-start.1
  494.0 1.6 copy-start.4
  496.0 88.4 %copy-start.3 = (bf16[512,256]{1,0:T(8,128)(2,1)S(1)}, bf16[512,256]{1,0:T(8,128)(2,1)}, u32[]{:S(2)}) copy-start(bf16[512,256]{1,0:T(8,128)(2,1)} %param.6) | copy-start | bytes 786436
  499.2 161.7 %copy-start.7 = (f32[2048]{0:T(1024)S(1)}, f32[2048]{0:T(1024)}, u32[]{:S(2)}) copy-start(f32[2048]{0:T(1024)} %param.8) | copy-start | bytes 24580
  499.2 159.5 %all-gather.5.cloned.1.call-start = ((), (), s32[]{:S(2)}) async-start(), calls=%async_computation.4 | async-start | bytes 2359296 | tf_op jit(solution)/shard_map/all_gather | solution.py:82
  586.2 174.0 %reduce-scatter.5.cloned.1.call-start = ((), (), s32[]{:S(2)}) async-start(), calls=%async_computation.5 | async-start | bytes 2359296 | tf_op jit(solution)/shard_map/reduce_scatter | solution.py:92
  658.7 2.2 copy-start.2
  669.0 91.2 %copy-start = (bf16[512,256]{1,0:T(8,128)(2,1)S(1)}, bf16[512,256]{1,0:T(8,128)(2,1)}, u32[]{:S(2)}) copy-start(bf16[512,256]{1,0:T(8,128)(2,1)} %add_convert_fusion.1) | copy-start | bytes 786436
Sparse Core Ops, SparseCore 0:
  11.2 78.4 all-gather.2
  499.3 85.0 reduce-scatter.2
  587.5 71.1 all-gather.4
  669.2 91.0 reduce-scatter.4
Sparse Core Ops, SparseCore 1:
  18.0 459.8 all-reduce.2
where the time goes:
time: 770 us; the launch traced here: 769 us
  waiting for transfers between devices  711 us (92%)
  between operations  16.7 us (2%)
  matrix products  14.3 us (2%)
  other arithmetic  12 us (2%)
  local copies, waits for them, and re-layouts  10.1 us (1%)
    psum x1, waiting for transfers between devices, spread(): return lax.psum(block, axis)  386 us
    reduce_scatter x1, waiting for transfers between devices, on_device(): lax.psum_scatter(ffn_part.astype(jnp.bfloat16), 'narrow', scatter_dimensi...  91.2 us
    reduce_scatter x1, waiting for transfers between devices, on_device(): lax.psum_scatter(partial_value.astype(jnp.bfloat16), 'narrow', scatter_di...  85.2 us
    all_gather x1, waiting for transfers between devices, on_device(): stream_full = lax.all_gather(stream, 'narrow', axis=1, tiled=True)  72.4 us
    all_gather x1, waiting for transfers between devices, on_device(): cell_full = lax.all_gather(cell_rows, 'narrow', axis=1, tiled=True)  71.7 us
  transfers between devices with their start and end apart: 7, of which 6 were waited for; matrix products, arithmetic and copies ran while one was open for 1% of the time, Pallas kernels for 0%

commit v1 on v0

v1 whole, which is shorter than its diff:
```python
import functools

import jax
import jax.numpy as jnp
from jax import lax
from jax.experimental import pallas as pl
from jax.experimental.pallas import tpu as pltpu
from jax.sharding import PartitionSpec as P

HD = 128
BLK = 128
NET_BLOCKS = 32
NZ = 16
NW = 64
NN = 8
UP = 8
DOWN = 7
epsilon = 1e-05

BF = jnp.bfloat16
F32 = jnp.float32
VM = pl.BlockSpec(memory_space=pltpu.VMEM)
SM = pl.BlockSpec(memory_space=pltpu.SMEM)
DMA = pltpu.SemaphoreType.DMA
LIMIT = 60 * 1024 * 1024


def remote(src, dst, send, recv, wide, narrow):
    return pltpu.make_async_remote_copy(
        src_ref=src, dst_ref=dst, send_sem=send, recv_sem=recv,
        device_id=(wide, narrow), device_id_type=pl.DeviceIdType.MESH,
    )


def greet(devices):
    barrier = pltpu.get_barrier_semaphore()
    for wide, narrow in devices:
        pl.semaphore_signal(
            barrier, inc=1, device_id=(wide, narrow), device_id_type=pl.DeviceIdType.MESH
        )
    pl.semaphore_wait(barrier, len(devices))


def loop(low, high, body):
    def step(s, carry):
        body(s)
        return carry

    lax.fori_loop(low, high, step, 0)


def panels_and_cells(
    cell, panel, slot, gath, out0, out1, out2,
    cbuf, rsp, rsm, ysend, yrecv,
    own_sem, csem, nsend, nrecv, psend, precv, msend, mrecv, ysem,
    gpsend, gprecv, gmsend, gmrecv, xsend, xrecv,
):
    outs = (out0, out1, out2)
    w = lax.axis_index("wide")
    n = lax.axis_index("narrow")
    core = w % 2
    z = (w // 2) % NZ
    yl = w // (2 * NZ)
    chip = w // 2

    def at_z(zz):
        return (yl * NZ + (zz + NZ) % NZ) * 2 + core

    above, below = at_z(z + 1), at_z(z - 1)
    partner = w + 1 - 2 * core
    across = (w + 2 * NZ) % NW
    peers = [(n + k) % NN for k in range(1, NN)]
    greet(
        [(partner, n), (above, n), (below, n), (across, n)] + [(w, p) for p in peers]
    )
    to_partner = remote(panel.at[:, 1 - core], cbuf, csem.at[0], csem.at[1], partner, n)
    to_partner.start()
    columns = gath.at[:, pl.ds(pl.multiple_of(n * 256, 256), 256)]
    own = pltpu.make_async_copy(cell, columns, own_sem)
    own.start()
    sends = []
    for k in range(1, NN):
        copy = remote(cell, columns, nsend.at[k - 1], nrecv.at[k - 1], w, peers[k - 1])
        copy.start()
        sends.append(copy)
    to_partner.wait_recv()

    slots = [slot[i] for i in range(3)]

    def chip_data(i, j):
        return jnp.where(slots[i] % 2 == core, panel[j, core], cbuf[j])

    def up(s, i):
        return remote(rsp.at[s, i], rsp.at[s + 1, i], psend.at[s, i], precv.at[s, i], above, n)

    def down(s, i):
        return remote(rsm.at[s, i], rsm.at[s + 1, i], msend.at[s, i], mrecv.at[s, i], below, n)

    for i in range(3):
        rsp[0, i] = chip_data(i, (z + UP) % NZ)
        up(0, i).start()
        rsm[0, i] = chip_data(i, (z + NZ - DOWN) % NZ)
        down(0, i).start()

    def merge_up(s, i):
        up(s - 1, i).wait_recv()
        mine = chip_data(i, (z + UP - s) % NZ)
        rsp[s, i] = jnp.where(slots[i] // 2 == chip, mine, rsp[s, i])
        up(s, i).start()

    def merge_down(s, i):
        down(s - 1, i).wait_recv()
        mine = chip_data(i, (z + NZ - DOWN + s) % NZ)
        rsm[s, i] = jnp.where(slots[i] // 2 == chip, mine, rsm[s, i])
        down(s, i).start()

    def both(s):
        for i in range(3):
            merge_up(s, i)
            merge_down(s, i)

    loop(1, DOWN, both)
    for i in range(3):
        merge_up(UP - 1, i)

    def swap(i):
        return remote(ysend.at[i], yrecv.at[i], ysem.at[0, i], ysem.at[1, i], across, n)

    for i in range(3):
        up(UP - 1, i).wait_recv()
        down(DOWN - 1, i).wait_recv()
        behind = (z - (slots[i] // 2) % NZ + NZ) % NZ
        ring = jnp.where(behind <= UP, rsp[UP, i], rsm[DOWN, i])
        ysend[i] = jnp.where(slots[i] // 2 == chip, chip_data(i, z), ring)
        swap(i).start()

    def gather_up(s, i):
        part = outs[i].at[(z - s + NZ) % NZ, core]
        return remote(part, part, gpsend.at[s, i], gprecv.at[s, i], above, n)

    def gather_down(s, i):
        part = outs[i].at[(z + s) % NZ, core]
        return remote(part, part, gmsend.at[s, i], gmrecv.at[s, i], below, n)

    def hand(order, chunk, i):
        part = outs[i].at[(chunk + NZ) % NZ, core]
        return remote(part, part, xsend.at[order, i], xrecv.at[order, i], partner, n)

    for i in range(3):
        swap(i).wait_recv()
        outs[i][z, core] = jnp.where(slots[i] // (2 * NZ) == yl, ysend[i], yrecv[i])
        gather_up(0, i).start()
        gather_down(0, i).start()
        hand(0, z, i).start()

    def relay_up(s, i):
        gather_up(s - 1, i).wait_recv()
        gather_up(s, i).start()
        hand(s, z - s, i).start()

    def relay_down(s, i):
        gather_down(s - 1, i).wait_recv()
        gather_down(s, i).start()
        hand(UP + s, z + s, i).start()

    def relay(s):
        for i in range(3):
            relay_up(s, i)
            relay_down(s, i)

    loop(1, DOWN, relay)
    for i in range(3):
        relay_up(DOWN, i)
    for i in range(3):
        gather_up(UP - 1, i).wait_recv()
        hand(UP, z - UP, i).start()
        gather_down(DOWN - 1, i).wait_recv()
        hand(UP + DOWN, z + DOWN, i).start()

    own.wait()
    to_partner.wait_send()
    for copy in sends:
        copy.wait()

    def finish(s):
        for i in range(3):
            up(s, i).wait_send()
            gather_up(s, i).wait_send()

            @pl.when(s < DOWN)
            def _():
                down(s, i).wait_send()
                gather_down(s, i).wait_send()

    loop(0, UP, finish)
    for i in range(3):
        swap(i).wait_send()

    def handed(order):
        for i in range(3):
            hand(order, z, i).wait()

    loop(0, NZ, handed)


def gather_all(cell_rows, panel, panel_slot):
    rows, width = cell_rows.shape
    piece = (64, 512)
    big = jax.ShapeDtypeStruct((NZ, 2, 64, 512), BF)
    gath, *outs = pl.pallas_call(
        panels_and_cells,
        name="panels_and_cells",
        out_shape=[jax.ShapeDtypeStruct((rows, width * NN), BF), big, big, big],
        in_specs=[VM, VM, SM],
        out_specs=[VM] * 4,
        scratch_shapes=[
            pltpu.VMEM((NZ,) + piece, BF),
            pltpu.VMEM((UP + 1, 3) + piece, BF),
            pltpu.VMEM((DOWN + 1, 3) + piece, BF),
            pltpu.VMEM((3,) + piece, BF),
            pltpu.VMEM((3,) + piece, BF),
            DMA, DMA((2,)), DMA((NN - 1,)), DMA((NN - 1,)),
            DMA((UP, 3)), DMA((UP, 3)), DMA((DOWN, 3)), DMA((DOWN, 3)), DMA((2, 3)),
            DMA((UP, 3)), DMA((UP, 3)), DMA((DOWN, 3)), DMA((DOWN, 3)),
            DMA((NZ, 3)), DMA((NZ, 3)),
        ],
        compiler_params=pltpu.CompilerParams(
            collective_id=0, has_side_effects=True, vmem_limit_bytes=LIMIT
        ),
    )(cell_rows, panel.reshape((NZ, 2, 64, 512)), panel_slot)
    return gath, [o.reshape(2048, 512) for o in outs]


def scatter_rows(part, got, send, recv, own_sem, w, n, peers):
    def columns(p):
        return part.at[:, pl.ds(pl.multiple_of(p * 256, 256), 256)]

    copies = []
    for k in range(1, NN):
        copy = remote(
            columns(peers[k - 1]), got.at[k - 1], send.at[k - 1], recv.at[k - 1], w, peers[k - 1]
        )
        copy.start()
        copies.append(copy)
    own = pltpu.make_async_copy(columns(n), got.at[NN - 1], own_sem)
    own.start()
    own.wait()
    for copy in copies:
        copy.wait()


def summed(base, got, rows):
    total = got[0, rows].astype(F32)
    for k in range(1, NN):
        total = total + got[k, rows].astype(F32)
    return (base[rows].astype(F32) + total).astype(BF)


def reduce_and_gather(
    part, cell, stream, gath, got, send, recv, own_sem, send2, recv2
):
    w = lax.axis_index("wide")
    n = lax.axis_index("narrow")
    peers = [(n + k) % NN for k in range(1, NN)]
    greet([(w, p) for p in peers])
    scatter_rows(part, got, send, recv, own_sem, w, n, peers)

    def block(r):
        rows = pl.ds(pl.multiple_of(r * 64, 64), 64)
        stream[rows] = summed(cell, got, rows)

    loop(0, 8, block)
    columns = gath.at[:, pl.ds(pl.multiple_of(n * 256, 256), 256)]
    own = pltpu.make_async_copy(stream, columns, own_sem)
    own.start()
    copies = []
    for k in range(1, NN):
        copy = remote(stream, columns, send2.at[k - 1], recv2.at[k - 1], w, peers[k - 1])
        copy.start()
        copies.append(copy)
    own.wait()
    for copy in copies:
        copy.wait()


def reduce_only(part, base, encoded, got, send, recv, own_sem):
    w = lax.axis_index("wide")
    n = lax.axis_index("narrow")
    peers = [(n + k) % NN for k in range(1, NN)]
    greet([(w, p) for p in peers])
    scatter_rows(part, got, send, recv, own_sem, w, n, peers)

    def block(r):
        rows = pl.ds(pl.multiple_of(r * 64, 64), 64)
        encoded[rows] = summed(base, got, rows)

    loop(0, 8, block)


def call_reduce_and_gather(part, cell):
    rows, width = cell.shape
    sems = DMA((NN - 1,))
    return pl.pallas_call(
        reduce_and_gather,
        name="reduce_and_gather",
        out_shape=[
            jax.ShapeDtypeStruct((rows, width), BF),
            jax.ShapeDtypeStruct((rows, width * NN), BF),
        ],
        in_specs=[VM] * 2,
        out_specs=[VM] * 2,
        scratch_shapes=[pltpu.VMEM((NN, rows, width), BF), sems, sems, DMA, sems, sems],
        compiler_params=pltpu.CompilerParams(
            collective_id=1, has_side_effects=True, vmem_limit_bytes=LIMIT
        ),
    )(part, cell)


def call_reduce_only(part, base):
    rows, width = base.shape
    sems = DMA((NN - 1,))
    return pl.pallas_call(
        reduce_only,
        name="reduce_only",
        out_shape=jax.ShapeDtypeStruct((rows, width), BF),
        in_specs=[VM] * 2,
        out_specs=VM,
        scratch_shapes=[pltpu.VMEM((NN, rows, width), BF), sems, sems, DMA],
        compiler_params=pltpu.CompilerParams(
            collective_id=2, has_side_effects=True, vmem_limit_bytes=LIMIT
        ),
    )(part, base)


def extended(shard, axis, width):
    size, length = (lax.axis_size(axis), shard.shape[0])
    up = [(i, (i + 1) % size) for i in range(size - 1)]
    down = [(j, i) for i, j in up]
    before = lax.ppermute(shard[length - width :], axis, up)
    after = lax.ppermute(shard[:width], axis, down)
    return jnp.concatenate([before, shard, after], axis=0)


def rms_scale(values, gain):
    mean_square = jnp.mean(values * values, axis=-1, keepdims=True)
    return values * lax.rsqrt(mean_square + epsilon) * gain


def block_mask(layout, query_index):
    wanted = query_index[:, None] + jnp.arange(5, dtype=jnp.int32)[None, :] - 2
    return jnp.any(layout[:, :, None] == wanted[:, None, :], axis=1)


def on_device(cell_rows, attn_gain, ffn_gain, panels, panel_slot, layout):
    row_count = cell_rows.shape[0]
    block_count = row_count // BLK
    cell_full, (attn_panel, up_panel, down_panel) = gather_all(cell_rows, panels[0], panel_slot)
    normed = rms_scale(cell_full.astype(F32), attn_gain).astype(BF)
    projected = jnp.dot(
        normed, attn_panel[:, : 3 * HD], preferred_element_type=F32
    ).astype(BF)
    key_window = extended(projected[:, HD:], "wide", 2 * BLK)
    pair_blocks = key_window.reshape(block_count + 4, BLK, 2, HD)
    stacked = jnp.stack([pair_blocks[o : o + block_count] for o in range(5)], axis=1)
    query_index = (
        lax.axis_index("wide") * block_count
        + jnp.arange(block_count, dtype=jnp.int32)
        + block_count // 2
    ) % NET_BLOCKS
    allowed = block_mask(layout, query_index)
    queries = projected[:, :HD].reshape(block_count, BLK, HD)
    scores = jnp.einsum(
        "bqc,bokc->bqok", queries, stacked[:, :, :, 0, :], preferred_element_type=F32
    ) * HD ** (-0.5)
    lifted = jnp.where(allowed[:, None, :, None], jnp.exp(scores), F32(0.0))
    weights = (lifted / jnp.sum(lifted, axis=(2, 3), keepdims=True)).astype(BF)
    head_out = jnp.einsum(
        "bqok,bokc->bqc", weights, stacked[:, :, :, 1, :], preferred_element_type=F32
    ).astype(BF)
    partial_value = lax.dot_general(
        head_out.reshape(row_count, HD), attn_panel[:, 3 * HD :],
        (((1,), (1,)), ((), ())), preferred_element_type=F32,
    ).astype(BF)
    stream, stream_full = call_reduce_and_gather(partial_value, cell_rows)
    normed_ffn = rms_scale(stream_full.astype(F32), ffn_gain).astype(BF)
    hidden = jax.nn.gelu(
        jnp.dot(normed_ffn, up_panel, preferred_element_type=F32), approximate=False
    ).astype(BF)
    ffn_part = lax.dot_general(
        hidden, down_panel, (((1,), (1,)), ((), ())), preferred_element_type=F32
    ).astype(BF)
    return call_reduce_only(ffn_part, stream)


def solution(mesh):
    return jax.shard_map(
        on_device,
        mesh=mesh,
        in_specs=(P("wide", "narrow"), P(), P(), P("wide", None, "narrow"), P(), P("wide", None)),
        out_specs=P("wide", "narrow"),
        check_vma=False,
    )
```

time: 770 us -> 235 us (0.31)
  waiting for transfers between devices: 711 us -> 1.55 us
  Pallas kernels: 0 us -> 204 us
  between operations: 16.7 us -> 0.23 us
    psum x1 -> x0, waiting for transfers between devices: 386 us -> none  [spread(): return lax.psum(block, axis)]
    pallas_call x0 -> x3, Pallas kernels: none -> 204 us  [the longest x1 99.1 us: gather_all(): pl.pallas_call(panels_and_cells, name='panels_and_cells', out_shape=[jax....]
    reduce_scatter x2 -> x0, waiting for transfers between devices: 176 us -> none  [the longest x1 91.2 us: on_device(): lax.psum_scatter(ffn_part.astype(jnp.bfloat16), 'narrow', scatter_dimensi...]
    all_gather x2 -> x0, waiting for transfers between devices: 144 us -> none  [the longest x1 72.4 us: on_device(): stream_full = lax.all_gather(stream, 'narrow', axis=1, tiled=True)]
  transfers between devices with their start and end apart: 7 -> 2, of which waited for: 6 -> 2; matrix products, arithmetic and copies ran while one was open for 1% -> 0% of each run, Pallas kernels for 0% -> 0%
where the time goes in v1:
time: 235 us; the launch traced here: 234 us
  Pallas kernels  204 us (87%)
  matrix products  14.7 us (6%)
  starting transfers between devices  5.56 us (2%)
  other arithmetic  4.7 us (2%)
  local copies, waits for them, and re-layouts  2.88 us (1%)
    pallas_call x1, Pallas kernels, gather_all(): pl.pallas_call(panels_and_cells, name='panels_and_cells', out_shape=[jax....  99.1 us
    pallas_call x1, Pallas kernels, call_reduce_and_gather(): pl.pallas_call(reduce_and_gather, name='reduce_and_gather', out_shape=[ja...  61.4 us
    pallas_call x1, Pallas kernels, call_reduce_only(): pl.pallas_call(reduce_only, name='reduce_only', out_shape=jax.ShapeDtypeS...  43.5 us
    dot_general x1, matrix products, on_device(): lax.dot_general(hidden, down_panel, (((1,), (1,)), ((), ())), preferred_e...  8.09 us
  transfers between devices with their start and end apart: 2, of which 2 were waited for; matrix products, arithmetic and copies ran while one was open for 0% of the time, Pallas kernels for 0%

profile of v1, /device:TPU:1, one launch (start us, length us, event | category | flops | bytes accessed | tf_op | source)
XLA Modules:
  0.0 233.6 jit_solution(9517814177088065647)
XLA Ops:
  0.0 0.0 copy-start.4
  0.0 99.1 %panels_and_cells.1 = (bf16[512,2048]{1,0:T(8,128)(2,1)}, bf16[16,2,64,512]{3,2,1,0:T(8,128)(2,1)}, bf16[16,2,64,512]{3,2,1,0:T(8,128)(2,1)}, bf16[16,2,64,512]{3,2,1,0:T(8,128)(2,1)}) custom-call(bf16[512,256]{1,0:T(8,128)(2,1)} %cell.3, bf16[16,2,64,512]{3,2,1,0:T(8,128)(2,1)} %bitcast.27, s32[64]{0:T(128)} %slot.1), custom_call_target="tpu_custom_call" | custom-call | tf_op jit(solution)/shard_map/panels_and_cells/pallas_call | solution.py:210
  99.1 0.0 copy-start.1
  99.1 2.2 fusion
  101.3 0.0 copy-done.4
  101.3 0.0 copy-done.1
  101.3 0.0 copy-start.3
  101.3 2.7 %fusion.17 = bf16[512,384]{1,0:T(8,128)(2,1)S(1)} fusion(bf16[2048,512]{1,0:T(8,128)(2,1)} %bitcast.29, bf16[512,2048]{1,0:T(8,128)(2,1)S(1)} %copy-done.1, f32[2048]{0:T(1024)S(1)} %copy-done.4, f32[512]{0:T(512)S(1)} %add_rsqrt_fusion.1), kind=kOutput, calls=%fused_computation.24 | convolution fusion | flops 809697280 | bytes 4073472 | tf_op jit(solution)/shard_map/dot_general | solution.py:359
  104.1 0.0 copy-start.2
  104.1 2.1 collective-permute-start.1
  106.2 3.5 %collective-permute-start = (bf16[256,256]{1,0:T(8,128)(2,1)S(1)}, bf16[256,256]{1,0:T(8,128)(2,1)S(1)}, u32[]{:S(2)}, u32[]{:S(2)}) collective-permute-start(bf16[256,256]{1,0:T(8,128)(2,1)S(1)} %get-tuple-element.20), channel_id=1, source_target_pairs={{0,8},{8,16},{16,24},{24,32},{32,40},{40,48},{48,56},{56,64},{64,7... | collective-permute-start | bytes 393224 | tf_op jit(solution)/shard_map/ppermute | solution.py:339
  109.7 0.1 add_add_fusion
  109.8 0.0 copy-done.3
  109.8 0.1 copy.13
  109.9 0.1 stack.20
  110.0 0.1 compare_reduce_fusion
  110.0 0.3 collective-permute-done.1
  110.4 1.2 collective-permute-done
  111.6 0.1 pad_maximum_fusion
  111.7 0.1 stack.22
  111.7 0.1 stack.21
  111.8 0.0 copy-done.2
  111.8 0.0 slice-start
  111.8 0.1 stack.18
  111.9 0.1 stack.19
  112.0 0.1 copy_dynamic-update-slice_fusion.3
  112.1 0.1 copy_dynamic-update-slice_fusion.2
  112.2 0.1 copy_dynamic-update-slice_fusion.1
  112.3 0.1 copy_dynamic-update-slice_fusion
  112.3 0.4 slice-done
  112.7 0.4 fusion.102
  113.1 0.4 fusion.22
  113.6 3.1 %convolution_convert_fusion.part = bf16[512,2048]{1,0:T(8,128)(2,1)} fusion(bf16[512,128]{1,0:T(8,128)(2,1)S(1)} %bitcast.31, bf16[2048,512]{1,0:T(8,128)(2,1)} %bitcast.30), kind=kOutput, calls=%fused_computation.10 | convolution fusion | flops 269484032 | bytes 2752512 | tf_op jit(solution)/shard_map/dot_general | solution.py:380
  116.7 0.0 copy-start.5
  116.7 61.4 %reduce_and_gather.1 = (bf16[512,256]{1,0:T(8,128)(2,1)}, bf16[512,2048]{1,0:T(8,128)(2,1)}) custom-call(bf16[512,2048]{1,0:T(8,128)(2,1)} %convolution_convert_fusion.part, bf16[512,256]{1,0:T(8,128)(2,1)} %cell.3), custom_call_target="tpu_custom_call" | custom-call | tf_op jit(solution)/shard_map/reduce_and_gather/pallas_call | solution.py:303
  178.1 0.0 copy-start
  178.1 2.2 fusion.3
  180.3 0.0 copy-done.5
  180.3 0.0 copy-done
  180.3 8.1 %convolution_convert_fusion.1.part = bf16[512,2048]{1,0:T(8,128)(2,1)} fusion(bf16[2048,512]{1,0:T(8,128)(2,1)} %bitcast.33, bf16[2048,512]{1,0:T(8,128)(2,1)} %bitcast.32, bf16[512,2048]{1,0:T(8,128)(2,1)S(1)} %copy-done, f32[2048]{0:T(1024)S(1)} %copy-done.5, f32[512]{0:T(512)S(1)} %add_rsqrt_fusion), kind=kOutput, calls=%fused_computation.11 | convolution fusion | flops 2169765888 | bytes 8398848 | tf_op jit(solution)/shard_map/dot_general | solution.py:389
  188.4 43.5 %reduce_only.1 = bf16[512,256]{1,0:T(8,128)(2,1)} custom-call(bf16[512,2048]{1,0:T(8,128)(2,1)} %convolution_convert_fusion.1.part, bf16[512,256]{1,0:T(8,128)(2,1)} %get-tuple-element.16.base), custom_call_target="tpu_custom_call" | custom-call | tf_op jit(solution)/shard_map/reduce_only/pallas_call | solution.py:322
  232.0 1.7 copy.33
  (6 shorter events, 0.1 us)
Async XLA Ops:
  0.0 101.3 %copy-start.4 = (f32[2048]{0:T(1024)S(1)}, f32[2048]{0:T(1024)}, u32[]{:S(2)}) copy-start(f32[2048]{0:T(1024)} %param.7) | copy-start | bytes 24580
  99.1 2.3 copy-start.1
  101.3 8.5 %copy-start.3 = (s32[4,3]{1,0:T(4,128)S(1)}, s32[4,3]{1,0:T(4,128)}, u32[]{:S(2)}) copy-start(s32[4,3]{1,0:T(4,128)} %param.11) | copy-start | bytes 148
  104.1 7.8 %copy-start.2 = (bf16[512,384]{1,0:T(8,128)(2,1)}, bf16[512,384]{1,0:T(8,128)(2,1)S(1)}, u32[]{:S(2)}) copy-start(bf16[512,384]{1,0:T(8,128)(2,1)S(1)} %fusion.17) | copy-start | bytes 1179652
  104.1 6.3 %collective-permute-start.1 = (bf16[256,256]{1,0:T(8,128)(2,1)S(1)}, bf16[256,256]{1,0:T(8,128)(2,1)S(1)}, u32[]{:S(2)}, u32[]{:S(2)}) collective-permute-start(bf16[256,256]{1,0:T(8,128)(2,1)S(1)} %get-tuple-element.19), channel_id=1, source_target_pairs={{8,0},{16,8},{24,16},{32,24},{40,32},{48,40},{56,48},{64,56},{72,6... | collective-permute-start | bytes 393224 | tf_op jit(solution)/shard_map/ppermute | solution.py:340
  106.2 5.4 %collective-permute-start = (bf16[256,256]{1,0:T(8,128)(2,1)S(1)}, bf16[256,256]{1,0:T(8,128)(2,1)S(1)}, u32[]{:S(2)}, u32[]{:S(2)}) collective-permute-start(bf16[256,256]{1,0:T(8,128)(2,1)S(1)} %get-tuple-element.20), channel_id=1, source_target_pairs={{0,8},{8,16},{16,24},{24,32},{32,40},{40,48},{48,56},{56,64},{64,7... | collective-permute-start | bytes 393224 | tf_op jit(solution)/shard_map/ppermute | solution.py:339
  111.8 0.9 slice-start
  116.7 63.6 %copy-start.5 = (f32[2048]{0:T(1024)S(1)}, f32[2048]{0:T(1024)}, u32[]{:S(2)}) copy-start(f32[2048]{0:T(1024)} %param.8) | copy-start | bytes 24580
  178.1 2.3 copy-start

commit v2 on v1

v2 whole, which is shorter than its diff:
```python
import functools

import jax
import jax.numpy as jnp
from jax import lax
from jax.experimental import pallas as pl
from jax.experimental.pallas import tpu as pltpu
from jax.sharding import PartitionSpec as P

HD = 128
BLK = 128
NET_BLOCKS = 32
NZ = 16
NW = 64
NN = 8
UP = 8
DOWN = 7
epsilon = 1e-05

BF = jnp.bfloat16
F32 = jnp.float32
VM = pl.BlockSpec(memory_space=pltpu.VMEM)
SM = pl.BlockSpec(memory_space=pltpu.SMEM)
DMA = pltpu.SemaphoreType.DMA
LIMIT = 60 * 1024 * 1024


def remote(src, dst, send, recv, wide, narrow):
    return pltpu.make_async_remote_copy(
        src_ref=src, dst_ref=dst, send_sem=send, recv_sem=recv,
        device_id=(wide, narrow), device_id_type=pl.DeviceIdType.MESH,
    )


def greet(devices):
    barrier = pltpu.get_barrier_semaphore()
    for wide, narrow in devices:
        pl.semaphore_signal(
            barrier, inc=1, device_id=(wide, narrow), device_id_type=pl.DeviceIdType.MESH
        )
    pl.semaphore_wait(barrier, len(devices))


def loop(low, high, body):
    def step(s, carry):
        body(s)
        return carry

    lax.fori_loop(low, high, step, 0)


class Spread:
    def __init__(self, panel, slots, outs, bufs, sems, w, n):
        self.panel, self.slots, self.outs = panel, slots, outs
        self.cbuf, self.rsp, self.rsm, self.ysend, self.yrecv = bufs
        (self.csem, self.psend, self.precv, self.msend, self.mrecv, self.ysem, self.gpsend,
         self.gprecv, self.gmsend, self.gmrecv, self.xsend, self.xrecv) = sems
        self.n, self.core, self.chip = n, w % 2, w // 2
        self.z, self.yl = (w // 2) % NZ, w // (2 * NZ)

        def at_z(zz):
            return (self.yl * NZ + (zz + NZ) % NZ) * 2 + self.core

        self.above, self.below = at_z(self.z + 1), at_z(self.z - 1)
        self.partner = w + 1 - 2 * self.core
        self.across = (w + 2 * NZ) % NW
        self.parts = panel.shape[2]
        self.streams = range(len(outs) * self.parts)
        self.neighbours = [(d, n) for d in (self.partner, self.above, self.below, self.across)]

    def owner(self, i):
        return self.slots[i // self.parts]

    def chip_data(self, i, j):
        part = i % self.parts
        return jnp.where(
            self.owner(i) % 2 == self.core,
            self.panel[j, self.core, part],
            self.cbuf[j, part],
        )

    def here(self, i, mine, other):
        return jnp.where(self.owner(i) // 2 == self.chip, mine, other)

    def up(self, s, i):
        return remote(
            self.rsp.at[s, i], self.rsp.at[s + 1, i],
            self.psend.at[s, i], self.precv.at[s, i], self.above, self.n,
        )

    def down(self, s, i):
        return remote(
            self.rsm.at[s, i], self.rsm.at[s + 1, i],
            self.msend.at[s, i], self.mrecv.at[s, i], self.below, self.n,
        )

    def place(self, chunk, i):
        return self.outs[i // self.parts].at[(chunk + NZ) % NZ, self.core, i % self.parts]

    def gather_up(self, s, i):
        part = self.place(self.z - s, i)
        return remote(part, part, self.gpsend.at[s, i], self.gprecv.at[s, i], self.above, self.n)

    def gather_down(self, s, i):
        part = self.place(self.z + s, i)
        return remote(part, part, self.gmsend.at[s, i], self.gmrecv.at[s, i], self.below, self.n)

    def hand(self, order, chunk, i):
        part = self.place(chunk, i)
        return remote(
            part, part, self.xsend.at[order, i], self.xrecv.at[order, i], self.partner, self.n
        )

    def swap(self, i):
        return remote(
            self.ysend.at[i], self.yrecv.at[i],
            self.ysem.at[0, i], self.ysem.at[1, i], self.across, self.n,
        )

    def to_partner(self):
        return remote(
            self.panel.at[:, 1 - self.core], self.cbuf,
            self.csem.at[0], self.csem.at[1], self.partner, self.n,
        )

    def reduce(self):
        z = self.z
        self.to_partner().wait_recv()
        for i in self.streams:
            self.rsp[0, i] = self.chip_data(i, (z + UP) % NZ)
            self.up(0, i).start()
            self.rsm[0, i] = self.chip_data(i, (z + NZ - DOWN) % NZ)
            self.down(0, i).start()

        def merge_up(s, i):
            self.up(s - 1, i).wait_recv()
            mine = self.chip_data(i, (z + UP - s) % NZ)
            self.rsp[s, i] = self.here(i, mine, self.rsp[s, i])
            self.up(s, i).start()

        def merge_down(s, i):
            self.down(s - 1, i).wait_recv()
            mine = self.chip_data(i, (z + NZ - DOWN + s) % NZ)
            self.rsm[s, i] = self.here(i, mine, self.rsm[s, i])
            self.down(s, i).start()

        def both(s):
            for i in self.streams:
                merge_up(s, i)
                merge_down(s, i)

        loop(1, DOWN, both)
        for i in self.streams:
            merge_up(UP - 1, i)
        for i in self.streams:
            self.up(UP - 1, i).wait_recv()
            self.down(DOWN - 1, i).wait_recv()
            behind = (z - (self.owner(i) // 2) % NZ + NZ) % NZ
            ring = jnp.where(behind <= UP, self.rsp[UP, i], self.rsm[DOWN, i])
            self.ysend[i] = self.here(i, self.chip_data(i, z), ring)
            self.swap(i).start()

    def gather(self):
        z = self.z
        for i in self.streams:
            self.swap(i).wait_recv()
            self.outs[i // self.parts][z, self.core, i % self.parts] = jnp.where(
                self.owner(i) // (2 * NZ) == self.yl, self.ysend[i], self.yrecv[i]
            )
            self.gather_up(0, i).start()
            self.gather_down(0, i).start()
            self.hand(0, z, i).start()

        def relay_up(s, i):
            self.gather_up(s - 1, i).wait_recv()
            self.gather_up(s, i).start()
            self.hand(s, z - s, i).start()

        def relay_down(s, i):
            self.gather_down(s - 1, i).wait_recv()
            self.gather_down(s, i).start()
            self.hand(UP + s, z + s, i).start()

        def relay(s):
            for i in self.streams:
                relay_up(s, i)
                relay_down(s, i)

        loop(1, DOWN, relay)
        for i in self.streams:
            relay_up(DOWN, i)
        for i in self.streams:
            self.gather_up(UP - 1, i).wait_recv()
            self.hand(UP, z - UP, i).start()
            self.gather_down(DOWN - 1, i).wait_recv()
            self.hand(UP + DOWN, z + DOWN, i).start()

    def finish(self):
        self.to_partner().wait_send()

        def sent(s):
            for i in self.streams:
                self.up(s, i).wait_send()
                self.gather_up(s, i).wait_send()

        def sent_down(s):
            for i in self.streams:
                self.down(s, i).wait_send()
                self.gather_down(s, i).wait_send()

        def handed(order):
            for i in self.streams:
                self.hand(order, self.z, i).wait()

        loop(0, UP, sent)
        loop(0, DOWN, sent_down)
        for i in self.streams:
            self.swap(i).wait_send()
        loop(0, NZ, handed)


def spread_scratch(count, parts):
    streams = count * parts
    piece = (64 // parts, 512)
    bufs = [
        pltpu.VMEM((NZ, parts) + piece, BF),
        pltpu.VMEM((UP + 1, streams) + piece, BF),
        pltpu.VMEM((DOWN + 1, streams) + piece, BF),
        pltpu.VMEM((streams,) + piece, BF),
        pltpu.VMEM((streams,) + piece, BF),
    ]
    ups, downs = DMA((UP, streams)), DMA((DOWN, streams))
    sems = [
        DMA((2,)), ups, ups, downs, downs, DMA((2, streams)), ups, ups, downs, downs,
        DMA((NZ, streams)), DMA((NZ, streams)),
    ]
    return bufs + sems


N_BUFS = 5
N_SPREAD = 17


def attn_and_cells(cell, panel, slot, gath, out, *scratch):
    own_sem, nsend, nrecv = scratch[N_SPREAD:]
    w = lax.axis_index("wide")
    n = lax.axis_index("narrow")
    spread = Spread(
        panel, [slot[0]], [out], scratch[:N_BUFS], scratch[N_BUFS:N_SPREAD], w, n
    )
    peers = [(n + k) % NN for k in range(1, NN)]
    greet(spread.neighbours + [(w, p) for p in peers])
    spread.to_partner().start()
    columns = gath.at[:, pl.ds(pl.multiple_of(n * 256, 256), 256)]
    own = pltpu.make_async_copy(cell, columns, own_sem)
    own.start()
    sends = []
    for k in range(1, NN):
        copy = remote(cell, columns, nsend.at[k - 1], nrecv.at[k - 1], w, peers[k - 1])
        copy.start()
        sends.append(copy)
    spread.reduce()
    spread.gather()
    own.wait()
    for copy in sends:
        copy.wait()
    spread.finish()


def call_attn_and_cells(cell_rows, panel, panel_slot):
    rows, width = cell_rows.shape
    parts = 2
    shape = (NZ, 2, parts, 64 // parts, 512)
    gath, out = pl.pallas_call(
        attn_and_cells,
        name="attn_and_cells",
        out_shape=[
            jax.ShapeDtypeStruct((rows, width * NN), BF),
            jax.ShapeDtypeStruct(shape, BF),
        ],
        in_specs=[VM, VM, SM],
        out_specs=[VM] * 2,
        scratch_shapes=spread_scratch(1, parts) + [DMA, DMA((NN - 1,)), DMA((NN - 1,))],
        compiler_params=pltpu.CompilerParams(
            collective_id=0, has_side_effects=True, vmem_limit_bytes=LIMIT
        ),
    )(cell_rows, panel.reshape(shape), panel_slot)
    return gath, out.reshape(2048, 512)


def scatter_rows(part, got, send, recv, own_sem, w, n, peers):
    def columns(p):
        return part.at[:, pl.ds(pl.multiple_of(p * 256, 256), 256)]

    copies = []
    for k in range(1, NN):
        copy = remote(
            columns(peers[k - 1]), got.at[k - 1], send.at[k - 1], recv.at[k - 1], w, peers[k - 1]
        )
        copy.start()
        copies.append(copy)
    own = pltpu.make_async_copy(columns(n), got.at[NN - 1], own_sem)
    own.start()
    return copies + [own]


def summed(base, got, rows):
    total = got[0, rows].astype(F32)
    for k in range(1, NN):
        total = total + got[k, rows].astype(F32)
    return (base[rows].astype(F32) + total).astype(BF)


def reduce_and_gather(part, cell, panel, slot, stream, gath, out0, out1, *scratch):
    got, send, recv, own_sem, send2, recv2 = scratch[N_SPREAD:]
    w = lax.axis_index("wide")
    n = lax.axis_index("narrow")
    spread = Spread(
        panel, [slot[1], slot[2]], [out0, out1],
        scratch[:N_BUFS], scratch[N_BUFS:N_SPREAD], w, n,
    )
    peers = [(n + k) % NN for k in range(1, NN)]
    greet(spread.neighbours + [(w, p) for p in peers])
    spread.to_partner().start()
    parts = scatter_rows(part, got, send, recv, own_sem, w, n, peers)
    spread.reduce()
    for copy in parts:
        copy.wait()

    def block(r):
        rows = pl.ds(pl.multiple_of(r * 64, 64), 64)
        stream[rows] = summed(cell, got, rows)

    loop(0, 8, block)
    columns = gath.at[:, pl.ds(pl.multiple_of(n * 256, 256), 256)]
    own = pltpu.make_async_copy(stream, columns, own_sem)
    own.start()
    copies = []
    for k in range(1, NN):
        copy = remote(stream, columns, send2.at[k - 1], recv2.at[k - 1], w, peers[k - 1])
        copy.start()
        copies.append(copy)
    spread.gather()
    own.wait()
    for copy in copies:
        copy.wait()
    spread.finish()


def reduce_only(part, base, encoded, got, send, recv, own_sem):
    w = lax.axis_index("wide")
    n = lax.axis_index("narrow")
    peers = [(n + k) % NN for k in range(1, NN)]
    greet([(w, p) for p in peers])
    for copy in scatter_rows(part, got, send, recv, own_sem, w, n, peers):
        copy.wait()

    def block(r):
        rows = pl.ds(pl.multiple_of(r * 64, 64), 64)
        encoded[rows] = summed(base, got, rows)

    loop(0, 8, block)


def call_reduce_and_gather(part, cell, panel, panel_slot):
    rows, width = cell.shape
    sems = DMA((NN - 1,))
    parts = 1
    shape = (NZ, 2, parts, 64 // parts, 512)
    stream, gath, *outs = pl.pallas_call(
        reduce_and_gather,
        name="reduce_and_gather",
        out_shape=[
            jax.ShapeDtypeStruct((rows, width), BF),
            jax.ShapeDtypeStruct((rows, width * NN), BF),
            jax.ShapeDtypeStruct(shape, BF),
            jax.ShapeDtypeStruct(shape, BF),
        ],
        in_specs=[VM, VM, VM, SM],
        out_specs=[VM] * 4,
        scratch_shapes=spread_scratch(2, parts)
        + [pltpu.VMEM((NN, rows, width), BF), sems, sems, DMA, sems, sems],
        compiler_params=pltpu.CompilerParams(
            collective_id=1, has_side_effects=True, vmem_limit_bytes=LIMIT
        ),
    )(part, cell, panel.reshape(shape), panel_slot)
    return [stream, gath] + [o.reshape(2048, 512) for o in outs]


def call_reduce_only(part, base):
    rows, width = base.shape
    sems = DMA((NN - 1,))
    return pl.pallas_call(
        reduce_only,
        name="reduce_only",
        out_shape=jax.ShapeDtypeStruct((rows, width), BF),
        in_specs=[VM] * 2,
        out_specs=VM,
        scratch_shapes=[pltpu.VMEM((NN, rows, width), BF), sems, sems, DMA],
        compiler_params=pltpu.CompilerParams(
            collective_id=2, has_side_effects=True, vmem_limit_bytes=LIMIT
        ),
    )(part, base)


def extended(shard, axis, width):
    size, length = (lax.axis_size(axis), shard.shape[0])
    up = [(i, (i + 1) % size) for i in range(size - 1)]
    down = [(j, i) for i, j in up]
    before = lax.ppermute(shard[length - width :], axis, up)
    after = lax.ppermute(shard[:width], axis, down)
    return jnp.concatenate([before, shard, after], axis=0)


def rms_scale(values, gain):
    mean_square = jnp.mean(values * values, axis=-1, keepdims=True)
    return values * lax.rsqrt(mean_square + epsilon) * gain


def block_mask(layout, query_index):
    wanted = query_index[:, None] + jnp.arange(5, dtype=jnp.int32)[None, :] - 2
    return jnp.any(layout[:, :, None] == wanted[:, None, :], axis=1)


def on_device(cell_rows, attn_gain, ffn_gain, panels, panel_slot, layout):
    row_count = cell_rows.shape[0]
    block_count = row_count // BLK
    cell_full, attn_panel = call_attn_and_cells(cell_rows, panels[0], panel_slot)
    normed = rms_scale(cell_full.astype(F32), attn_gain).astype(BF)
    projected = jnp.dot(
        normed, attn_panel[:, : 3 * HD], preferred_element_type=F32
    ).astype(BF)
    key_window = extended(projected[:, HD:], "wide", 2 * BLK)
    pair_blocks = key_window.reshape(block_count + 4, BLK, 2, HD)
    stacked = jnp.stack([pair_blocks[o : o + block_count] for o in range(5)], axis=1)
    query_index = (
        lax.axis_index("wide") * block_count
        + jnp.arange(block_count, dtype=jnp.int32)
        + block_count // 2
    ) % NET_BLOCKS
    allowed = block_mask(layout, query_index)
    queries = projected[:, :HD].reshape(block_count, BLK, HD)
    scores = jnp.einsum(
        "bqc,bokc->bqok", queries, stacked[:, :, :, 0, :], preferred_element_type=F32
    ) * HD ** (-0.5)
    lifted = jnp.where(allowed[:, None, :, None], jnp.exp(scores), F32(0.0))
    weights = (lifted / jnp.sum(lifted, axis=(2, 3), keepdims=True)).astype(BF)
    head_out = jnp.einsum(
        "bqok,bokc->bqc", weights, stacked[:, :, :, 1, :], preferred_element_type=F32
    ).astype(BF)
    partial_value = lax.dot_general(
        head_out.reshape(row_count, HD), attn_panel[:, 3 * HD :],
        (((1,), (1,)), ((), ())), preferred_element_type=F32,
    ).astype(BF)
    stream, stream_full, up_panel, down_panel = call_reduce_and_gather(
        partial_value, cell_rows, panels[0], panel_slot
    )
    normed_ffn = rms_scale(stream_full.astype(F32), ffn_gain).astype(BF)
    hidden = jax.nn.gelu(
        jnp.dot(normed_ffn, up_panel, preferred_element_type=F32), approximate=False
    ).astype(BF)
    ffn_part = lax.dot_general(
        hidden, down_panel, (((1,), (1,)), ((), ())), preferred_element_type=F32
    ).astype(BF)
    return call_reduce_only(ffn_part, stream)


def solution(mesh):
    return jax.shard_map(
        on_device,
        mesh=mesh,
        in_specs=(P("wide", "narrow"), P(), P(), P("wide", None, "narrow"), P(), P("wide", None)),
        out_specs=P("wide", "narrow"),
        check_vma=False,
    )
```

time: 235 us -> 244 us (1.038); the launches traced: 234 us -> 239 us
  Pallas kernels: 204 us -> 209 us
    pallas_call x1, Pallas kernels: 99.1 us -> 80.3 us  [call_attn_and_cells(): pl.pallas_call(attn_and_cells, name='attn_and_cells', out_shape=[jax.Shap...]
    pallas_call x1, Pallas kernels: 61.4 us -> 79.9 us  [call_reduce_and_gather(): pl.pallas_call(reduce_and_gather, name='reduce_and_gather', out_shape=[ja...]
    pallas_call x1, Pallas kernels: 43.5 us -> 49.3 us  [call_reduce_only(): pl.pallas_call(reduce_only, name='reduce_only', out_shape=jax.ShapeDtypeS...]
where the time goes in v2:
time: 244 us; the launch traced here: 239 us
  Pallas kernels  209 us (86%)
  matrix products  14.7 us (6%)
  starting transfers between devices  5.56 us (2%)
  other arithmetic  4.7 us (2%)
  local copies, waits for them, and re-layouts  2.88 us (1%)
    pallas_call x1, Pallas kernels, call_attn_and_cells(): pl.pallas_call(attn_and_cells, name='attn_and_cells', out_shape=[jax.Shap...  80.3 us
    pallas_call x1, Pallas kernels, call_reduce_and_gather(): pl.pallas_call(reduce_and_gather, name='reduce_and_gather', out_shape=[ja...  79.9 us
    pallas_call x1, Pallas kernels, call_reduce_only(): pl.pallas_call(reduce_only, name='reduce_only', out_shape=jax.ShapeDtypeS...  49.3 us
    dot_general x1, matrix products, on_device(): lax.dot_general(hidden, down_panel, (((1,), (1,)), ((), ())), preferred_e...  8.1 us
  transfers between devices with their start and end apart: 2, of which 2 were waited for; matrix products, arithmetic and copies ran while one was open for 0% of the time, Pallas kernels for 0%

profile of v2, /device:TPU:1, one launch (start us, length us, event | category | flops | bytes accessed | tf_op | source)
XLA Modules:
  0.0 239.1 jit_solution(3419743895940922690)
XLA Ops:
  0.0 0.0 copy-start.4
  0.0 80.3 %attn_and_cells.1 = (bf16[512,2048]{1,0:T(8,128)(2,1)}, bf16[16,2,2,32,512]{4,3,2,1,0:T(8,128)(2,1)}) custom-call(bf16[512,256]{1,0:T(8,128)(2,1)} %cell.3, bf16[16,2,2,32,512]{4,3,2,1,0:T(8,128)(2,1)} %bitcast.28, s32[64]{0:T(128)} %slot.3), custom_call_target="tpu_custom_call" | custom-call | tf_op jit(solution)/shard_map/attn_and_cells/pallas_call | solution.py:274
  80.3 0.0 copy-start.1
  80.3 2.2 fusion
  82.5 0.0 copy-done.4
  82.5 0.0 copy-done.1
  82.5 0.0 copy-start.3
  82.6 2.7 %fusion.17 = bf16[512,384]{1,0:T(8,128)(2,1)S(1)} fusion(bf16[2048,512]{1,0:T(8,128)(2,1)} %bitcast.31, bf16[512,2048]{1,0:T(8,128)(2,1)S(1)} %copy-done.1, f32[2048]{0:T(1024)S(1)} %copy-done.4, f32[512]{0:T(512)S(1)} %add_rsqrt_fusion.1), kind=kOutput, calls=%fused_computation.24 | convolution fusion | flops 809697280 | bytes 4073472 | tf_op jit(solution)/shard_map/dot_general | solution.py:430
  85.3 0.0 copy-start.2
  85.3 2.1 collective-permute-start.1
  87.4 3.5 %collective-permute-start = (bf16[256,256]{1,0:T(8,128)(2,1)S(1)}, bf16[256,256]{1,0:T(8,128)(2,1)S(1)}, u32[]{:S(2)}, u32[]{:S(2)}) collective-permute-start(bf16[256,256]{1,0:T(8,128)(2,1)S(1)} %get-tuple-element.20), channel_id=1, source_target_pairs={{0,8},{8,16},{16,24},{24,32},{32,40},{40,48},{48,56},{56,64},{64,7... | collective-permute-start | bytes 393224 | tf_op jit(solution)/shard_map/ppermute | solution.py:410
  90.9 0.1 add_add_fusion
  91.0 0.0 copy-done.3
  91.0 0.1 copy.13
  91.1 0.1 stack.20
  91.2 0.1 compare_reduce_fusion
  91.3 0.3 collective-permute-done.1
  91.6 1.2 collective-permute-done
  92.8 0.1 pad_maximum_fusion
  92.9 0.1 stack.22
  93.0 0.1 stack.21
  93.0 0.0 copy-done.2
  93.0 0.0 slice-start
  93.1 0.1 stack.18
  93.1 0.1 stack.19
  93.2 0.1 copy_dynamic-update-slice_fusion.3
  93.3 0.1 copy_dynamic-update-slice_fusion.2
  93.4 0.1 copy_dynamic-update-slice_fusion.1
  93.5 0.1 copy_dynamic-update-slice_fusion
  93.6 0.4 slice-done
  93.9 0.4 fusion.102
  94.4 0.4 fusion.22
  94.8 3.1 %convolution_convert_fusion.part = bf16[512,2048]{1,0:T(8,128)(2,1)} fusion(bf16[512,128]{1,0:T(8,128)(2,1)S(1)} %bitcast.33, bf16[2048,512]{1,0:T(8,128)(2,1)} %bitcast.32), kind=kOutput, calls=%fused_computation.10 | convolution fusion | flops 269484032 | bytes 2752512 | tf_op jit(solution)/shard_map/dot_general | solution.py:451
  97.9 79.9 %reduce_and_gather.1 = (bf16[512,256]{1,0:T(8,128)(2,1)}, bf16[512,2048]{1,0:T(8,128)(2,1)}, bf16[16,2,1,64,512]{4,3,2,1,0:T(8,128)(2,1)}, bf16[16,2,1,64,512]{4,3,2,1,0:T(8,128)(2,1)}) custom-call(bf16[512,2048]{1,0:T(8,128)(2,1)} %convolution_convert_fusion.part, bf16[512,256]{1,0:T(8,128)(2,1)} %cell.3, bf16[16,2,1,64,512]{4,3,2,1,0:T(8,128)(2,1)} %bitcast.29, ...), custom_call_target="tpu_custom_call" | custom-call | tf_op jit(solution)/shard_map/reduce_and_gather/pallas_call | solution.py:370
  177.8 0.0 copy-start
  177.8 0.0 copy-start.5
  177.8 2.2 fusion.3
  180.0 0.0 copy-done
  180.0 0.0 copy-done.5
  180.1 8.1 %convolution_convert_fusion.1.part = bf16[512,2048]{1,0:T(8,128)(2,1)} fusion(bf16[2048,512]{1,0:T(8,128)(2,1)} %bitcast.35, bf16[2048,512]{1,0:T(8,128)(2,1)} %bitcast.34, bf16[512,2048]{1,0:T(8,128)(2,1)S(1)} %copy-done, f32[2048]{0:T(1024)S(1)} %copy-done.5, f32[512]{0:T(512)S(1)} %add_rsqrt_fusion), kind=kOutput, calls=%fused_computation.11 | convolution fusion | flops 2169765888 | bytes 8398848 | tf_op jit(solution)/shard_map/dot_general | solution.py:462
  188.2 49.3 %reduce_only.1 = bf16[512,256]{1,0:T(8,128)(2,1)} custom-call(bf16[512,2048]{1,0:T(8,128)(2,1)} %convolution_convert_fusion.1.part, bf16[512,256]{1,0:T(8,128)(2,1)} %get-tuple-element.16.base), custom_call_target="tpu_custom_call" | custom-call | tf_op jit(solution)/shard_map/reduce_only/pallas_call | solution.py:393
  237.5 1.7 copy.33
  (6 shorter events, 0.1 us)
Async XLA Ops:
  0.0 82.5 %copy-start.4 = (f32[2048]{0:T(1024)S(1)}, f32[2048]{0:T(1024)}, u32[]{:S(2)}) copy-start(f32[2048]{0:T(1024)} %param.7) | copy-start | bytes 24580
  80.3 2.3 copy-start.1
  82.5 8.5 %copy-start.3 = (s32[4,3]{1,0:T(4,128)S(1)}, s32[4,3]{1,0:T(4,128)}, u32[]{:S(2)}) copy-start(s32[4,3]{1,0:T(4,128)} %param.11) | copy-start | bytes 148
  85.3 7.8 %copy-start.2 = (bf16[512,384]{1,0:T(8,128)(2,1)}, bf16[512,384]{1,0:T(8,128)(2,1)S(1)}, u32[]{:S(2)}) copy-start(bf16[512,384]{1,0:T(8,128)(2,1)S(1)} %fusion.17) | copy-start | bytes 1179652
  85.3 6.3 %collective-permute-start.1 = (bf16[256,256]{1,0:T(8,128)(2,1)S(1)}, bf16[256,256]{1,0:T(8,128)(2,1)S(1)}, u32[]{:S(2)}, u32[]{:S(2)}) collective-permute-start(bf16[256,256]{1,0:T(8,128)(2,1)S(1)} %get-tuple-element.19), channel_id=1, source_target_pairs={{8,0},{16,8},{24,16},{32,24},{40,32},{48,40},{56,48},{64,56},{72,6... | collective-permute-start | bytes 393224 | tf_op jit(solution)/shard_map/ppermute | solution.py:411
  87.4 5.4 %collective-permute-start = (bf16[256,256]{1,0:T(8,128)(2,1)S(1)}, bf16[256,256]{1,0:T(8,128)(2,1)S(1)}, u32[]{:S(2)}, u32[]{:S(2)}) collective-permute-start(bf16[256,256]{1,0:T(8,128)(2,1)S(1)} %get-tuple-element.20), channel_id=1, source_target_pairs={{0,8},{8,16},{16,24},{24,32},{32,40},{40,48},{48,56},{56,64},{64,7... | collective-permute-start | bytes 393224 | tf_op jit(solution)/shard_map/ppermute | solution.py:410
  93.0 0.9 slice-start
  177.8 2.3 copy-start
  177.8 2.3 copy-start.5

commit v3 on v1

--- a/solution.py
+++ b/solution.py
@@ -231,75 +231,204 @@
     return gath, [o.reshape(2048, 512) for o in outs]
 
 
-def scatter_rows(part, got, send, recv, own_sem, w, n, peers):
-    def columns(p):
-        return part.at[:, pl.ds(pl.multiple_of(p * 256, 256), 256)]
-
-    copies = []
-    for k in range(1, NN):
-        copy = remote(
-            columns(peers[k - 1]), got.at[k - 1], send.at[k - 1], recv.at[k - 1], w, peers[k - 1]
+class Narrow:
+    def __init__(self):
+        self.w, self.n = lax.axis_index("wide"), lax.axis_index("narrow")
+        self.x, self.h = self.n // 2, self.n % 2
+        self.right = (self.w, (self.n + 2) % NN)
+        self.left = (self.w, (self.n + NN - 2) % NN)
+        self.pair = (self.w, self.n + 1 - 2 * self.h)
+        self.devices = [self.right, self.left, self.pair]
+
+
+CH = 4
+ROWS = 512 // CH
+
+
+def rows_of(c):
+    return pl.ds(c * ROWS, ROWS)
+
+
+class Sum:
+    def __init__(self, net, part, bufs, sems):
+        self.net, self.part = net, part
+        self.far, self.relay, self.near_r, self.near_l, self.ysend, self.yrecv = bufs
+        self.fs, self.fr, self.rs, self.rr, self.ls, self.lr, self.ys, self.yr = sems
+
+    def block(self, x, c):
+        start = pl.multiple_of(((x + 4) % 4) * 512, 512)
+        return self.part.at[rows_of(c), pl.ds(start, 512)]
+
+    def to_far(self, c):
+        target = self.net.right if c % 2 == 0 else self.net.left
+        return remote(
+            self.block(self.net.x + 2, c), self.far.at[c], self.fs.at[c], self.fr.at[c], *target
         )
-        copy.start()
-        copies.append(copy)
-    own = pltpu.make_async_copy(columns(n), got.at[NN - 1], own_sem)
-    own.start()
-    own.wait()
-    for copy in copies:
-        copy.wait()
-
-
-def summed(base, got, rows):
-    total = got[0, rows].astype(F32)
-    for k in range(1, NN):
-        total = total + got[k, rows].astype(F32)
-    return (base[rows].astype(F32) + total).astype(BF)
-
-
-def reduce_and_gather(
-    part, cell, stream, gath, got, send, recv, own_sem, send2, recv2
-):
-    w = lax.axis_index("wide")
-    n = lax.axis_index("narrow")
-    peers = [(n + k) % NN for k in range(1, NN)]
-    greet([(w, p) for p in peers])
-    scatter_rows(part, got, send, recv, own_sem, w, n, peers)
-
-    def block(r):
-        rows = pl.ds(pl.multiple_of(r * 64, 64), 64)
-        stream[rows] = summed(cell, got, rows)
-
-    loop(0, 8, block)
-    columns = gath.at[:, pl.ds(pl.multiple_of(n * 256, 256), 256)]
+
+    def to_right(self, c):
+        source = self.relay.at[c] if c % 2 == 0 else self.block(self.net.x + 1, c)
+        return remote(source, self.near_r.at[c], self.rs.at[c], self.rr.at[c], *self.net.right)
+
+    def to_left(self, c):
+        source = self.relay.at[c] if c % 2 == 1 else self.block(self.net.x - 1, c)
+        return remote(source, self.near_l.at[c], self.ls.at[c], self.lr.at[c], *self.net.left)
+
+    def to_pair(self, c):
+        return remote(
+            self.ysend.at[c], self.yrecv.at[c], self.ys.at[c], self.yr.at[c], *self.net.pair
+        )
+
+    def start(self):
+        for c in range(CH):
+            self.to_far(c).start()
+
+    def forward(self, c):
+        self.to_far(c).wait_recv()
+        step = 1 if c % 2 == 0 else -1
+        mine = self.block(self.net.x + step, c)[...]
+        self.relay[c] = (mine.astype(F32) + self.far[c].astype(F32)).astype(BF)
+        self.to_right(c).start()
+        self.to_left(c).start()
+
+    def columns(self, c, h):
+        start = pl.multiple_of((self.net.x * 2 + h) * 256, 256)
+        cols = pl.ds(pl.multiple_of(h * 256, 256), 256)
+        total = self.part[rows_of(c), pl.ds(start, 256)].astype(F32)
+        total = total + self.near_r[c, :, cols].astype(F32)
+        return total + self.near_l[c, :, cols].astype(F32)
+
+    def cross(self, c):
+        self.to_right(c).wait_recv()
+        self.to_left(c).wait_recv()
+        self.ysend[c] = self.columns(c, 1 - self.net.h).astype(BF)
+        self.to_pair(c).start()
+
+    def total(self, c):
+        self.to_pair(c).wait_recv()
+        return self.columns(c, self.net.h) + self.yrecv[c].astype(F32)
+
+    def finish(self):
+        for c in range(CH):
+            self.to_far(c).wait_send()
+            self.to_right(c).wait_send()
+            self.to_left(c).wait_send()
+            self.to_pair(c).wait_send()
+
+
+SUM_SCRATCH = (
+    [pltpu.VMEM((CH, ROWS, 512), BF)] * 4
+    + [pltpu.VMEM((CH, ROWS, 256), BF)] * 2
+    + [DMA((CH,))] * 8
+)
+
+
+class Gather:
+    def __init__(self, net, piece, gath, sems):
+        self.net, self.piece, self.gath = net, piece, gath
+        self.ys, self.yr, self.rs, self.rr, self.ls, self.lr, self.fs, self.fr = sems
+
+    def place(self, x, q, c):
+        h = self.net.h if q == 0 else 1 - self.net.h
+        start = pl.multiple_of((((x + 4) % 4) * 2 + h) * 256, 256)
+        return self.gath.at[rows_of(c), pl.ds(start, 256)]
+
+    def source(self, q, c):
+        return self.piece.at[rows_of(c)] if q == 0 else self.place(self.net.x, 1, c)
+
+    def to_pair(self, c):
+        return remote(
+            self.source(0, c), self.place(self.net.x, 0, c),
+            self.ys.at[c], self.yr.at[c], *self.net.pair,
+        )
+
+    def to_right(self, q, c):
+        return remote(
+            self.source(q, c), self.place(self.net.x, q, c),
+            self.rs.at[q, c], self.rr.at[q, c], *self.net.right,
+        )
+
+    def to_left(self, q, c):
+        return remote(
+            self.source(q, c), self.place(self.net.x, q, c),
+            self.ls.at[q, c], self.lr.at[q, c], *self.net.left,
+        )
+
+    def onward(self, q, c):
+        step, target = (-1, self.net.right) if c % 2 == 0 else (1, self.net.left)
+        part = self.place(self.net.x + step, q, c)
+        return remote(part, part, self.fs.at[q, c], self.fr.at[q, c], *target)
+
+    def start(self, c):
+        self.to_pair(c).start()
+        self.to_right(0, c).start()
+        self.to_left(0, c).start()
+
+    def spread_pair(self, c):
+        self.to_pair(c).wait_recv()
+        self.to_right(1, c).start()
+        self.to_left(1, c).start()
+
+    def relay(self, q, c):
+        self.to_right(q, c).wait_recv()
+        self.to_left(q, c).wait_recv()
+        self.onward(q, c).start()
+
+    def finish(self):
+        for c in range(CH):
+            self.to_pair(c).wait_send()
+            for q in range(2):
+                self.to_right(q, c).wait_send()
+                self.to_left(q, c).wait_send()
+                self.onward(q, c).wait()
+
+
+GATHER_SCRATCH = [DMA((CH,))] * 2 + [DMA((2, CH))] * 6
+
+
+def reduce_and_gather(part, cell, stream, gath, own_sem, *scratch):
+    net = Narrow()
+    greet(net.devices)
+    add = Sum(net, part, scratch[:6], scratch[6:14])
+    spread = Gather(net, stream, gath, scratch[14:])
+    add.start()
+    for c in range(CH):
+        add.forward(c)
+    for c in range(CH):
+        add.cross(c)
+    columns = gath.at[:, pl.ds(pl.multiple_of(net.n * 256, 256), 256)]
+    for c in range(CH):
+        total = cell[rows_of(c)].astype(F32) + add.total(c)
+        stream[rows_of(c)] = total.astype(BF)
+        spread.start(c)
     own = pltpu.make_async_copy(stream, columns, own_sem)
     own.start()
-    copies = []
-    for k in range(1, NN):
-        copy = remote(stream, columns, send2.at[k - 1], recv2.at[k - 1], w, peers[k - 1])
-        copy.start()
-        copies.append(copy)
+    for c in range(CH):
+        spread.spread_pair(c)
+    for q in range(2):
+        for c in range(CH):
+            spread.relay(q, c)
     own.wait()
-    for copy in copies:
-        copy.wait()
-
-
-def reduce_only(part, base, encoded, got, send, recv, own_sem):
-    w = lax.axis_index("wide")
-    n = lax.axis_index("narrow")
-    peers = [(n + k) % NN for k in range(1, NN)]
-    greet([(w, p) for p in peers])
-    scatter_rows(part, got, send, recv, own_sem, w, n, peers)
-
-    def block(r):
-        rows = pl.ds(pl.multiple_of(r * 64, 64), 64)
-        encoded[rows] = summed(base, got, rows)
-
-    loop(0, 8, block)
+    add.finish()
+    spread.finish()
+
+
+def reduce_only(part, base, encoded, *scratch):
+    net = Narrow()
+    greet(net.devices)
+    add = Sum(net, part, scratch[:6], scratch[6:])
+    add.start()
+    for c in range(CH):
+        add.forward(c)
+    for c in range(CH):
+        add.cross(c)
+    for c in range(CH):
+        total = base[rows_of(c)].astype(F32) + add.total(c)
+        encoded[rows_of(c)] = total.astype(BF)
+    add.finish()
 
 
 def call_reduce_and_gather(part, cell):
     rows, width = cell.shape
-    sems = DMA((NN - 1,))
     return pl.pallas_call(
         reduce_and_gather,
         name="reduce_and_gather",
@@ -309,7 +438,7 @@
         ],
         in_specs=[VM] * 2,
         out_specs=[VM] * 2,
-        scratch_shapes=[pltpu.VMEM((NN, rows, width), BF), sems, sems, DMA, sems, sems],
+        scratch_shapes=[DMA] + SUM_SCRATCH + GATHER_SCRATCH,
         compiler_params=pltpu.CompilerParams(
             collective_id=1, has_side_effects=True, vmem_limit_bytes=LIMIT
         ),
@@ -318,14 +447,13 @@
 
 def call_reduce_only(part, base):
     rows, width = base.shape
-    sems = DMA((NN - 1,))
     return pl.pallas_call(
         reduce_only,
         name="reduce_only",
         out_shape=jax.ShapeDtypeStruct((rows, width), BF),
         in_specs=[VM] * 2,
         out_specs=VM,
-        scratch_shapes=[pltpu.VMEM((NN, rows, width), BF), sems, sems, DMA],
+        scratch_shapes=SUM_SCRATCH,
         compiler_params=pltpu.CompilerParams(
             collective_id=2, has_side_effects=True, vmem_limit_bytes=LIMIT
         ),

time: 235 us -> 199 us (0.85)
  Pallas kernels: 204 us -> 168 us
    pallas_call x1, Pallas kernels: 61.4 us -> 42.6 us  [call_reduce_and_gather(): pl.pallas_call(reduce_and_gather, name='reduce_and_gather', out_shape=[ja...]
    pallas_call x1, Pallas kernels: 43.5 us -> 26.8 us  [call_reduce_only(): pl.pallas_call(reduce_only, name='reduce_only', out_shape=jax.ShapeDtypeS...]
where the time goes in v3:
time: 199 us; the launch traced here: 198 us
  Pallas kernels  168 us (84%)
  matrix products  14.7 us (7%)
  starting transfers between devices  5.56 us (3%)
  other arithmetic  4.7 us (2%)
  local copies, waits for them, and re-layouts  2.88 us (1%)
    pallas_call x1, Pallas kernels, gather_all(): pl.pallas_call(panels_and_cells, name='panels_and_cells', out_shape=[jax....  99.1 us
    pallas_call x1, Pallas kernels, call_reduce_and_gather(): pl.pallas_call(reduce_and_gather, name='reduce_and_gather', out_shape=[ja...  42.6 us
    pallas_call x1, Pallas kernels, call_reduce_only(): pl.pallas_call(reduce_only, name='reduce_only', out_shape=jax.ShapeDtypeS...  26.8 us
    dot_general x1, matrix products, on_device(): lax.dot_general(hidden, down_panel, (((1,), (1,)), ((), ())), preferred_e...  8.08 us
    reduce_sum x2, other arithmetic, rms_scale(): mean_square = jnp.mean(values * values, axis=-1, keepdims=True)  4.45 us
  transfers between devices with their start and end apart: 2, of which 2 were waited for; matrix products, arithmetic and copies ran while one was open for 0% of the time, Pallas kernels for 0%

profile of v3, /device:TPU:1, one launch (start us, length us, event | category | flops | bytes accessed | tf_op | source)
XLA Modules:
  0.0 198.1 jit_solution(2820030317988975226)
XLA Ops:
  0.0 0.0 copy-start.4
  0.0 99.1 %panels_and_cells.1 = (bf16[512,2048]{1,0:T(8,128)(2,1)}, bf16[16,2,64,512]{3,2,1,0:T(8,128)(2,1)}, bf16[16,2,64,512]{3,2,1,0:T(8,128)(2,1)}, bf16[16,2,64,512]{3,2,1,0:T(8,128)(2,1)}) custom-call(bf16[512,256]{1,0:T(8,128)(2,1)} %cell.3, bf16[16,2,64,512]{3,2,1,0:T(8,128)(2,1)} %bitcast.27, s32[64]{0:T(128)} %slot.1), custom_call_target="tpu_custom_call" | custom-call | tf_op jit(solution)/shard_map/panels_and_cells/pallas_call | solution.py:210
  99.1 0.0 copy-start.1
  99.1 2.2 %fusion = f32[512]{0:T(512)S(1)} fusion(bf16[512,2048]{1,0:T(8,128)(2,1)} %get-tuple-element.11), kind=kLoop, calls=%fused_computation.4 | loop fusion | flops 3145216 | bytes 2099200 | tf_op jit(solution)/shard_map/reduce_sum | solution.py:473
  101.3 0.0 copy-done.4
  101.3 0.0 copy-done.1
  101.3 0.0 copy-start.3
  101.3 2.7 %fusion.17 = bf16[512,384]{1,0:T(8,128)(2,1)S(1)} fusion(bf16[2048,512]{1,0:T(8,128)(2,1)} %bitcast.29, bf16[512,2048]{1,0:T(8,128)(2,1)S(1)} %copy-done.1, f32[2048]{0:T(1024)S(1)} %copy-done.4, f32[512]{0:T(512)S(1)} %add_rsqrt_fusion.1), kind=kOutput, calls=%fused_computation.24 | convolution fusion | flops 809697280 | bytes 4073472 | tf_op jit(solution)/shard_map/dot_general | solution.py:487
  104.1 0.0 copy-start.2
  104.1 2.1 %collective-permute-start.1 = (bf16[256,256]{1,0:T(8,128)(2,1)S(1)}, bf16[256,256]{1,0:T(8,128)(2,1)S(1)}, u32[]{:S(2)}, u32[]{:S(2)}) collective-permute-start(bf16[256,256]{1,0:T(8,128)(2,1)S(1)} %get-tuple-element.19), channel_id=1, source_target_pairs={{8,0},{16,8},{24,16},{32,24},{40,32},{48,40},{56,48},{64,56},{72,6... | collective-permute-start | bytes 393224 | tf_op jit(solution)/shard_map/ppermute | solution.py:468
  106.2 3.5 %collective-permute-start = (bf16[256,256]{1,0:T(8,128)(2,1)S(1)}, bf16[256,256]{1,0:T(8,128)(2,1)S(1)}, u32[]{:S(2)}, u32[]{:S(2)}) collective-permute-start(bf16[256,256]{1,0:T(8,128)(2,1)S(1)} %get-tuple-element.20), channel_id=1, source_target_pairs={{0,8},{8,16},{16,24},{24,32},{32,40},{40,48},{48,56},{56,64},{64,7... | collective-permute-start | bytes 393224 | tf_op jit(solution)/shard_map/ppermute | solution.py:467
  109.7 0.1 add_add_fusion
  109.8 0.0 copy-done.3
  109.8 0.1 copy.13
  109.9 0.1 stack.20
  110.0 0.1 compare_reduce_fusion
  110.0 0.3 collective-permute-done.1
  110.4 1.2 collective-permute-done
  111.6 0.1 pad_maximum_fusion
  111.7 0.1 stack.22
  111.7 0.1 stack.21
  111.8 0.0 copy-done.2
  111.8 0.0 slice-start
  111.8 0.1 stack.18
  111.9 0.1 stack.19
  112.0 0.1 copy_dynamic-update-slice_fusion.3
  112.1 0.1 copy_dynamic-update-slice_fusion.2
  112.2 0.1 copy_dynamic-update-slice_fusion.1
  112.3 0.1 copy_dynamic-update-slice_fusion
  112.3 0.4 slice-done
  112.7 0.4 fusion.102
  113.1 0.4 fusion.22
  113.6 3.1 %convolution_convert_fusion.part = bf16[512,2048]{1,0:T(8,128)(2,1)} fusion(bf16[512,128]{1,0:T(8,128)(2,1)S(1)} %bitcast.31, bf16[2048,512]{1,0:T(8,128)(2,1)} %bitcast.30), kind=kOutput, calls=%fused_computation.10 | convolution fusion | flops 269484032 | bytes 2752512 | tf_op jit(solution)/shard_map/dot_general | solution.py:508
  116.7 0.0 copy-start.5
  116.7 42.6 %reduce_and_gather.1 = (bf16[512,256]{1,0:T(8,128)(2,1)}, bf16[512,2048]{1,0:T(8,128)(2,1)}) custom-call(bf16[512,2048]{1,0:T(8,128)(2,1)} %convolution_convert_fusion.part, bf16[512,256]{1,0:T(8,128)(2,1)} %cell.3), custom_call_target="tpu_custom_call" | custom-call | tf_op jit(solution)/shard_map/reduce_and_gather/pallas_call | solution.py:432
  159.2 0.0 copy-start
  159.2 2.2 %fusion.3 = f32[512]{0:T(512)S(1)} fusion(bf16[512,2048]{1,0:T(8,128)(2,1)} %get-tuple-element.13), kind=kLoop, calls=%fused_computation.7 | loop fusion | flops 3145216 | bytes 2099200 | tf_op jit(solution)/shard_map/reduce_sum | solution.py:473
  161.5 0.0 copy-done.5
  161.5 0.0 copy-done
  161.5 8.1 %convolution_convert_fusion.1.part = bf16[512,2048]{1,0:T(8,128)(2,1)} fusion(bf16[2048,512]{1,0:T(8,128)(2,1)} %bitcast.33, bf16[2048,512]{1,0:T(8,128)(2,1)} %bitcast.32, bf16[512,2048]{1,0:T(8,128)(2,1)S(1)} %copy-done, f32[2048]{0:T(1024)S(1)} %copy-done.5, f32[512]{0:T(512)S(1)} %add_rsqrt_fusion), kind=kOutput, calls=%fused_computation.11 | convolution fusion | flops 2169765888 | bytes 8398848 | tf_op jit(solution)/shard_map/dot_general | solution.py:517
  169.6 26.8 %reduce_only.1 = bf16[512,256]{1,0:T(8,128)(2,1)} custom-call(bf16[512,2048]{1,0:T(8,128)(2,1)} %convolution_convert_fusion.1.part, bf16[512,256]{1,0:T(8,128)(2,1)} %get-tuple-element.16.base), custom_call_target="tpu_custom_call" | custom-call | tf_op jit(solution)/shard_map/reduce_only/pallas_call | solution.py:450
  196.4 1.7 copy.33
  (6 shorter events, 0.1 us)
Async XLA Ops:
  0.0 101.3 %copy-start.4 = (f32[2048]{0:T(1024)S(1)}, f32[2048]{0:T(1024)}, u32[]{:S(2)}) copy-start(f32[2048]{0:T(1024)} %param.7) | copy-start | bytes 24580
  99.1 2.3 %copy-start.1 = (bf16[512,2048]{1,0:T(8,128)(2,1)S(1)}, bf16[512,2048]{1,0:T(8,128)(2,1)}, u32[]{:S(2)}) copy-start(bf16[512,2048]{1,0:T(8,128)(2,1)} %get-tuple-element.11) | copy-start | bytes 6291460
  101.3 8.5 %copy-start.3 = (s32[4,3]{1,0:T(4,128)S(1)}, s32[4,3]{1,0:T(4,128)}, u32[]{:S(2)}) copy-start(s32[4,3]{1,0:T(4,128)} %param.11) | copy-start | bytes 148
  104.1 7.8 %copy-start.2 = (bf16[512,384]{1,0:T(8,128)(2,1)}, bf16[512,384]{1,0:T(8,128)(2,1)S(1)}, u32[]{:S(2)}) copy-start(bf16[512,384]{1,0:T(8,128)(2,1)S(1)} %fusion.17) | copy-start | bytes 1179652
  104.1 6.3 %collective-permute-start.1 = (bf16[256,256]{1,0:T(8,128)(2,1)S(1)}, bf16[256,256]{1,0:T(8,128)(2,1)S(1)}, u32[]{:S(2)}, u32[]{:S(2)}) collective-permute-start(bf16[256,256]{1,0:T(8,128)(2,1)S(1)} %get-tuple-element.19), channel_id=1, source_target_pairs={{8,0},{16,8},{24,16},{32,24},{40,32},{48,40},{56,48},{64,56},{72,6... | collective-permute-start | bytes 393224 | tf_op jit(solution)/shard_map/ppermute | solution.py:468
  106.2 5.4 %collective-permute-start = (bf16[256,256]{1,0:T(8,128)(2,1)S(1)}, bf16[256,256]{1,0:T(8,128)(2,1)S(1)}, u32[]{:S(2)}, u32[]{:S(2)}) collective-permute-start(bf16[256,256]{1,0:T(8,128)(2,1)S(1)} %get-tuple-element.20), channel_id=1, source_target_pairs={{0,8},{8,16},{16,24},{24,32},{32,40},{40,48},{48,56},{56,64},{64,7... | collective-permute-start | bytes 393224 | tf_op jit(solution)/shard_map/ppermute | solution.py:467
  111.8 0.9 slice-start
  116.7 44.8 %copy-start.5 = (f32[2048]{0:T(1024)S(1)}, f32[2048]{0:T(1024)}, u32[]{:S(2)}) copy-start(f32[2048]{0:T(1024)} %param.8) | copy-start | bytes 24580
  159.2 2.3 %copy-start = (bf16[512,2048]{1,0:T(8,128)(2,1)S(1)}, bf16[512,2048]{1,0:T(8,128)(2,1)}, u32[]{:S(2)}) copy-start(bf16[512,2048]{1,0:T(8,128)(2,1)} %get-tuple-element.13) | copy-start | bytes 6291460

commit v4 on v3

--- a/solution.py
+++ b/solution.py
@@ -49,32 +49,222 @@
     lax.fori_loop(low, high, step, 0)
 
 
-def panels_and_cells(
-    cell, panel, slot, gath, out0, out1, out2,
-    cbuf, rsp, rsm, ysend, yrecv,
-    own_sem, csem, nsend, nrecv, psend, precv, msend, mrecv, ysem,
-    gpsend, gprecv, gmsend, gmrecv, xsend, xrecv,
-):
-    outs = (out0, out1, out2)
-    w = lax.axis_index("wide")
-    n = lax.axis_index("narrow")
-    core = w % 2
-    z = (w // 2) % NZ
-    yl = w // (2 * NZ)
-    chip = w // 2
-
-    def at_z(zz):
-        return (yl * NZ + (zz + NZ) % NZ) * 2 + core
-
-    above, below = at_z(z + 1), at_z(z - 1)
-    partner = w + 1 - 2 * core
-    across = (w + 2 * NZ) % NW
+class Place:
+    def __init__(self):
+        self.w, self.n = lax.axis_index("wide"), lax.axis_index("narrow")
+        self.core, self.chip = self.w % 2, self.w // 2
+        self.z, self.yl = self.chip % NZ, self.w // (2 * NZ)
+        self.above = (self.at_z(self.z + 1), self.n)
+        self.below = (self.at_z(self.z - 1), self.n)
+        self.partner = (self.w + 1 - 2 * self.core, self.n)
+        self.across = ((self.w + 2 * NZ) % NW, self.n)
+
+    def at_z(self, zz):
+        return (self.yl * NZ + (zz + NZ) % NZ) * 2 + self.core
+
+
+class Pick:
+    def __init__(self, at, panel, slots, bufs, sems):
+        self.at, self.panel, self.slots = at, panel, slots
+        self.cbuf, self.rsp, self.rsm, self.ysend, self.yrecv = bufs
+        self.csem, self.psend, self.precv, self.msend, self.mrecv, self.ysem = sems
+        self.parts = panel.shape[2]
+        self.count = len(slots) * self.parts
+
+    def owner(self, i):
+        return self.slots[i // self.parts]
+
+    def chip_data(self, i, j):
+        part = i % self.parts
+        return jnp.where(
+            self.owner(i) % 2 == self.at.core,
+            self.panel[j, self.at.core, part],
+            self.cbuf[j, part],
+        )
+
+    def here(self, i, mine, other):
+        return jnp.where(self.owner(i) // 2 == self.at.chip, mine, other)
+
+    def up(self, s, i):
+        return remote(
+            self.rsp.at[s, i], self.rsp.at[s + 1, i],
+            self.psend.at[s, i], self.precv.at[s, i], *self.at.above,
+        )
+
+    def down(self, s, i):
+        return remote(
+            self.rsm.at[s, i], self.rsm.at[s + 1, i],
+            self.msend.at[s, i], self.mrecv.at[s, i], *self.at.below,
+        )
+
+    def swap(self, i):
+        return remote(
+            self.ysend.at[i], self.yrecv.at[i],
+            self.ysem.at[0, i], self.ysem.at[1, i], *self.at.across,
+        )
+
+    def to_partner(self):
+        return remote(
+            self.panel.at[:, 1 - self.at.core], self.cbuf,
+            self.csem.at[0], self.csem.at[1], *self.at.partner,
+        )
+
+    def begin(self, i):
+        self.rsp[0, i] = self.chip_data(i, (self.at.z + UP) % NZ)
+        self.up(0, i).start()
+        self.rsm[0, i] = self.chip_data(i, (self.at.z + NZ - DOWN) % NZ)
+        self.down(0, i).start()
+
+    def merge_up(self, s, i):
+        self.up(s - 1, i).wait_recv()
+        mine = self.chip_data(i, (self.at.z + UP - s) % NZ)
+        self.rsp[s, i] = self.here(i, mine, self.rsp[s, i])
+        self.up(s, i).start()
+
+    def merge_down(self, s, i):
+        self.down(s - 1, i).wait_recv()
+        mine = self.chip_data(i, (self.at.z + NZ - DOWN + s) % NZ)
+        self.rsm[s, i] = self.here(i, mine, self.rsm[s, i])
+        self.down(s, i).start()
+
+    def end(self, i):
+        self.up(UP - 1, i).wait_recv()
+        self.down(DOWN - 1, i).wait_recv()
+        behind = (self.at.z - (self.owner(i) // 2) % NZ + NZ) % NZ
+        ring = jnp.where(behind <= UP, self.rsp[UP, i], self.rsm[DOWN, i])
+        self.ysend[i] = self.here(i, self.chip_data(i, self.at.z), ring)
+        self.swap(i).start()
+
+    def result(self, i):
+        self.swap(i).wait_recv()
+        return jnp.where(
+            self.owner(i) // (2 * NZ) == self.at.yl, self.ysend[i], self.yrecv[i]
+        )
+
+    def finish(self):
+        self.to_partner().wait_send()
+
+        def sent(s):
+            for i in range(self.count):
+                self.up(s, i).wait_send()
+
+        def sent_down(s):
+            for i in range(self.count):
+                self.down(s, i).wait_send()
+
+        loop(0, UP, sent)
+        loop(0, DOWN, sent_down)
+        for i in range(self.count):
+            self.swap(i).wait_send()
+
+
+class Fan:
+    def __init__(self, at, outs, sems):
+        self.at, self.outs = at, outs
+        self.gpsend, self.gprecv, self.gmsend, self.gmrecv, self.xsend, self.xrecv = sems
+        self.parts = outs[0].shape[2]
+        self.streams = range(len(outs) * self.parts)
+
+    def place(self, chunk, i):
+        return self.outs[i // self.parts].at[(chunk + NZ) % NZ, self.at.core, i % self.parts]
+
+    def up(self, s, i, source=None):
+        part = self.place(self.at.z - s, i)
+        source = part if source is None else source
+        return remote(source, part, self.gpsend.at[s, i], self.gprecv.at[s, i], *self.at.above)
+
+    def down(self, s, i, source=None):
+        part = self.place(self.at.z + s, i)
+        source = part if source is None else source
+        return remote(source, part, self.gmsend.at[s, i], self.gmrecv.at[s, i], *self.at.below)
+
+    def hand(self, order, chunk, i, source=None):
+        part = self.place(chunk, i)
+        source = part if source is None else source
+        return remote(
+            source, part, self.xsend.at[order, i], self.xrecv.at[order, i], *self.at.partner
+        )
+
+    def begin(self, i, source=None):
+        self.up(0, i, source).start()
+        self.down(0, i, source).start()
+        self.hand(0, self.at.z, i, source).start()
+
+    def relay_up(self, s, i):
+        self.up(s - 1, i).wait_recv()
+        self.up(s, i).start()
+        self.hand(s, self.at.z - s, i).start()
+
+    def relay_down(self, s, i):
+        self.down(s - 1, i).wait_recv()
+        self.down(s, i).start()
+        self.hand(UP + s, self.at.z + s, i).start()
+
+    def relay(self, s):
+        for i in self.streams:
+            self.relay_up(s, i)
+            self.relay_down(s, i)
+
+    def last(self):
+        for i in self.streams:
+            self.relay_up(DOWN, i)
+
+    def end(self):
+        for i in self.streams:
+            self.up(UP - 1, i).wait_recv()
+            self.hand(UP, self.at.z - UP, i).start()
+            self.down(DOWN - 1, i).wait_recv()
+            self.hand(UP + DOWN, self.at.z + DOWN, i).start()
+
+    def finish(self):
+        def sent(s):
+            for i in self.streams:
+                self.up(s, i).wait_send()
+
+        def sent_down(s):
+            for i in self.streams:
+                self.down(s, i).wait_send()
+
+        def handed(order):
+            for i in self.streams:
+                self.hand(order, self.at.z, i).wait()
+
+        loop(0, UP, sent)
+        loop(0, DOWN, sent_down)
+        loop(0, NZ, handed)
+
+
+PARTS = 2
+
+
+def pick_scratch():
+    piece = (64 // PARTS, 512)
+    count = 3 * PARTS
+    ups, downs = DMA((UP, count)), DMA((DOWN, count))
+    return [
+        pltpu.VMEM((NZ, PARTS) + piece, BF),
+        pltpu.VMEM((UP + 1, count) + piece, BF),
+        pltpu.VMEM((DOWN + 1, count) + piece, BF),
+        pltpu.VMEM((count,) + piece, BF),
+        pltpu.VMEM((count,) + piece, BF),
+        DMA((2,)), ups, ups, downs, downs, DMA((2, count)),
+    ]
+
+
+def fan_scratch(count):
+    ups, downs, hands = DMA((UP, count)), DMA((DOWN, count)), DMA((NZ, count))
+    return [ups, ups, downs, downs, hands, hands]
+
+
+def panels_and_cells(cell, panel, slot, gath, out, shares, *scratch):
+    at = Place()
+    pick = Pick(at, panel, [slot[i] for i in range(3)], scratch[:5], scratch[5:11])
+    fan = Fan(at, [out], scratch[11:17])
+    own_sem, nsend, nrecv = scratch[17:]
+    w, n = at.w, at.n
     peers = [(n + k) % NN for k in range(1, NN)]
-    greet(
-        [(partner, n), (above, n), (below, n), (across, n)] + [(w, p) for p in peers]
-    )
-    to_partner = remote(panel.at[:, 1 - core], cbuf, csem.at[0], csem.at[1], partner, n)
-    to_partner.start()
+    greet([at.partner, at.above, at.below, at.across] + [(w, p) for p in peers])
+    pick.to_partner().start()
     columns = gath.at[:, pl.ds(pl.multiple_of(n * 256, 256), 256)]
     own = pltpu.make_async_copy(cell, columns, own_sem)
     own.start()
@@ -83,152 +273,71 @@
         copy = remote(cell, columns, nsend.at[k - 1], nrecv.at[k - 1], w, peers[k - 1])
         copy.start()
         sends.append(copy)
-    to_partner.wait_recv()
-
-    slots = [slot[i] for i in range(3)]
-
-    def chip_data(i, j):
-        return jnp.where(slots[i] % 2 == core, panel[j, core], cbuf[j])
-
-    def up(s, i):
-        return remote(rsp.at[s, i], rsp.at[s + 1, i], psend.at[s, i], precv.at[s, i], above, n)
-
-    def down(s, i):
-        return remote(rsm.at[s, i], rsm.at[s + 1, i], msend.at[s, i], mrecv.at[s, i], below, n)
-
-    for i in range(3):
-        rsp[0, i] = chip_data(i, (z + UP) % NZ)
-        up(0, i).start()
-        rsm[0, i] = chip_data(i, (z + NZ - DOWN) % NZ)
-        down(0, i).start()
-
-    def merge_up(s, i):
-        up(s - 1, i).wait_recv()
-        mine = chip_data(i, (z + UP - s) % NZ)
-        rsp[s, i] = jnp.where(slots[i] // 2 == chip, mine, rsp[s, i])
-        up(s, i).start()
-
-    def merge_down(s, i):
-        down(s - 1, i).wait_recv()
-        mine = chip_data(i, (z + NZ - DOWN + s) % NZ)
-        rsm[s, i] = jnp.where(slots[i] // 2 == chip, mine, rsm[s, i])
-        down(s, i).start()
+    first = range(2 * PARTS)
+    later = range(2 * PARTS, 3 * PARTS)
+    pick.to_partner().wait_recv()
+    for i in first:
+        pick.begin(i)
 
     def both(s):
-        for i in range(3):
-            merge_up(s, i)
-            merge_down(s, i)
+        for i in first:
+            pick.merge_up(s, i)
+            pick.merge_down(s, i)
 
     loop(1, DOWN, both)
-    for i in range(3):
-        merge_up(UP - 1, i)
-
-    def swap(i):
-        return remote(ysend.at[i], yrecv.at[i], ysem.at[0, i], ysem.at[1, i], across, n)
-
-    for i in range(3):
-        up(UP - 1, i).wait_recv()
-        down(DOWN - 1, i).wait_recv()
-        behind = (z - (slots[i] // 2) % NZ + NZ) % NZ
-        ring = jnp.where(behind <= UP, rsp[UP, i], rsm[DOWN, i])
-        ysend[i] = jnp.where(slots[i] // 2 == chip, chip_data(i, z), ring)
-        swap(i).start()
-
-    def gather_up(s, i):
-        part = outs[i].at[(z - s + NZ) % NZ, core]
-        return remote(part, part, gpsend.at[s, i], gprecv.at[s, i], above, n)
-
-    def gather_down(s, i):
-        part = outs[i].at[(z + s) % NZ, core]
-        return remote(part, part, gmsend.at[s, i], gmrecv.at[s, i], below, n)
-
-    def hand(order, chunk, i):
-        part = outs[i].at[(chunk + NZ) % NZ, core]
-        return remote(part, part, xsend.at[order, i], xrecv.at[order, i], partner, n)
-
-    for i in range(3):
-        swap(i).wait_recv()
-        outs[i][z, core] = jnp.where(slots[i] // (2 * NZ) == yl, ysend[i], yrecv[i])
-        gather_up(0, i).start()
-        gather_down(0, i).start()
-        hand(0, z, i).start()
-
-    def relay_up(s, i):
-        gather_up(s - 1, i).wait_recv()
-        gather_up(s, i).start()
-        hand(s, z - s, i).start()
-
-    def relay_down(s, i):
-        gather_down(s - 1, i).wait_recv()
-        gather_down(s, i).start()
-        hand(UP + s, z + s, i).start()
-
-    def relay(s):
-        for i in range(3):
-            relay_up(s, i)
-            relay_down(s, i)
-
-    loop(1, DOWN, relay)
-    for i in range(3):
-        relay_up(DOWN, i)
-    for i in range(3):
-        gather_up(UP - 1, i).wait_recv()
-        hand(UP, z - UP, i).start()
-        gather_down(DOWN - 1, i).wait_recv()
-        hand(UP + DOWN, z + DOWN, i).start()
-
+    for i in first:
+        pick.merge_up(UP - 1, i)
+    for i in first:
+        pick.end(i)
+    for i in range(PARTS):
+        out[at.z, at.core, i] = pick.result(i)
+        fan.begin(i)
+    for i in later:
+        pick.begin(i)
+
+    def mixed(s):
+        fan.relay(s)
+        for i in later:
+            pick.merge_up(s, i)
+            pick.merge_down(s, i)
+
+    loop(1, DOWN, mixed)
+    fan.last()
+    for i in later:
+        pick.merge_up(UP - 1, i)
+    fan.end()
+    for i in later:
+        pick.end(i)
+    for i in range(PARTS, 3 * PARTS):
+        shares[i - PARTS] = pick.result(i)
     own.wait()
-    to_partner.wait_send()
     for copy in sends:
         copy.wait()
-
-    def finish(s):
-        for i in range(3):
-            up(s, i).wait_send()
-            gather_up(s, i).wait_send()
-
-            @pl.when(s < DOWN)
-            def _():
-                down(s, i).wait_send()
-                gather_down(s, i).wait_send()
-
-    loop(0, UP, finish)
-    for i in range(3):
-        swap(i).wait_send()
-
-    def handed(order):
-        for i in range(3):
-            hand(order, z, i).wait()
-
-    loop(0, NZ, handed)
+    pick.finish()
+    fan.finish()
 
 
 def gather_all(cell_rows, panel, panel_slot):
     rows, width = cell_rows.shape
-    piece = (64, 512)
-    big = jax.ShapeDtypeStruct((NZ, 2, 64, 512), BF)
-    gath, *outs = pl.pallas_call(
+    shape = (NZ, 2, PARTS, 64 // PARTS, 512)
+    gath, out, shares = pl.pallas_call(
         panels_and_cells,
         name="panels_and_cells",
-        out_shape=[jax.ShapeDtypeStruct((rows, width * NN), BF), big, big, big],
+        out_shape=[
+            jax.ShapeDtypeStruct((rows, width * NN), BF),
+            jax.ShapeDtypeStruct(shape, BF),
+            jax.ShapeDtypeStruct((2 * PARTS, 64 // PARTS, 512), BF),
+        ],
         in_specs=[VM, VM, SM],
-        out_specs=[VM] * 4,
-        scratch_shapes=[
-            pltpu.VMEM((NZ,) + piece, BF),
-            pltpu.VMEM((UP + 1, 3) + piece, BF),
-            pltpu.VMEM((DOWN + 1, 3) + piece, BF),
-            pltpu.VMEM((3,) + piece, BF),
-            pltpu.VMEM((3,) + piece, BF),
-            DMA, DMA((2,)), DMA((NN - 1,)), DMA((NN - 1,)),
-            DMA((UP, 3)), DMA((UP, 3)), DMA((DOWN, 3)), DMA((DOWN, 3)), DMA((2, 3)),
-            DMA((UP, 3)), DMA((UP, 3)), DMA((DOWN, 3)), DMA((DOWN, 3)),
-            DMA((NZ, 3)), DMA((NZ, 3)),
-        ],
+        out_specs=[VM] * 3,
+        scratch_shapes=pick_scratch()
+        + fan_scratch(PARTS)
+        + [DMA, DMA((NN - 1,)), DMA((NN - 1,))],
         compiler_params=pltpu.CompilerParams(
             collective_id=0, has_side_effects=True, vmem_limit_bytes=LIMIT
         ),
-    )(cell_rows, panel.reshape((NZ, 2, 64, 512)), panel_slot)
-    return gath, [o.reshape(2048, 512) for o in outs]
+    )(cell_rows, panel.reshape(shape), panel_slot)
+    return gath, out.reshape(2048, 512), shares.reshape(2, 64, 512)
 
 
 class Narrow:
@@ -385,16 +494,28 @@
 GATHER_SCRATCH = [DMA((CH,))] * 2 + [DMA((2, CH))] * 6
 
 
-def reduce_and_gather(part, cell, stream, gath, own_sem, *scratch):
+def reduce_and_gather(part, cell, shares, stream, gath, out0, out1, own_sem, share_sem, *scratch):
     net = Narrow()
-    greet(net.devices)
+    at = Place()
+    greet(net.devices + [at.partner, at.above, at.below])
     add = Sum(net, part, scratch[:6], scratch[6:14])
-    spread = Gather(net, stream, gath, scratch[14:])
+    spread = Gather(net, stream, gath, scratch[14:22])
+    fan = Fan(at, [out0, out1], scratch[22:])
     add.start()
+    kept = []
+    for i in fan.streams:
+        fan.begin(i, shares.at[i])
+        copy = pltpu.make_async_copy(shares.at[i], fan.place(at.z, i), share_sem.at[i])
+        copy.start()
+        kept.append(copy)
     for c in range(CH):
         add.forward(c)
+        if c % 2 == 1:
+            fan.relay(c // 2 + 1)
     for c in range(CH):
         add.cross(c)
+        if c % 2 == 1:
+            fan.relay(c // 2 + 3)
     columns = gath.at[:, pl.ds(pl.multiple_of(net.n * 256, 256), 256)]
     for c in range(CH):
         total = cell[rows_of(c)].astype(F32) + add.total(c)
@@ -402,14 +523,22 @@
         spread.start(c)
     own = pltpu.make_async_copy(stream, columns, own_sem)
     own.start()
+    fan.relay(5)
     for c in range(CH):
         spread.spread_pair(c)
-    for q in range(2):
-        for c in range(CH):
-            spread.relay(q, c)
+    fan.relay(6)
+    for c in range(CH):
+        spread.relay(0, c)
+    fan.last()
+    for c in range(CH):
+        spread.relay(1, c)
+    fan.end()
     own.wait()
+    for copy in kept:
+        copy.wait()
     add.finish()
     spread.finish()
+    fan.finish()
 
 
 def reduce_only(part, base, encoded, *scratch):
@@ -427,22 +556,26 @@
     add.finish()
 
 
-def call_reduce_and_gather(part, cell):
+def call_reduce_and_gather(part, cell, shares):
     rows, width = cell.shape
-    return pl.pallas_call(
+    panel = jax.ShapeDtypeStruct((NZ, 2, 1, 64, 512), BF)
+    stream, gath, *outs = pl.pallas_call(
         reduce_and_gather,
         name="reduce_and_gather",
         out_shape=[
             jax.ShapeDtypeStruct((rows, width), BF),
             jax.ShapeDtypeStruct((rows, width * NN), BF),
+            panel,
+            panel,
         ],
-        in_specs=[VM] * 2,
-        out_specs=[VM] * 2,
-        scratch_shapes=[DMA] + SUM_SCRATCH + GATHER_SCRATCH,
+        in_specs=[VM] * 3,
+        out_specs=[VM] * 4,
+        scratch_shapes=[DMA, DMA((2,))] + SUM_SCRATCH + GATHER_SCRATCH + fan_scratch(2),
         compiler_params=pltpu.CompilerParams(
             collective_id=1, has_side_effects=True, vmem_limit_bytes=LIMIT
         ),
-    )(part, cell)
+    )(part, cell, shares)
+    return [stream, gath] + [o.reshape(2048, 512) for o in outs]
 
 
 def call_reduce_only(part, base):
@@ -482,7 +615,7 @@
 def on_device(cell_rows, attn_gain, ffn_gain, panels, panel_slot, layout):
     row_count = cell_rows.shape[0]
     block_count = row_count // BLK
-    cell_full, (attn_panel, up_panel, down_panel) = gather_all(cell_rows, panels[0], panel_slot)
+    cell_full, attn_panel, shares = gather_all(cell_rows, panels[0], panel_slot)
     normed = rms_scale(cell_full.astype(F32), attn_gain).astype(BF)
     projected = jnp.dot(
         normed, attn_panel[:, : 3 * HD], preferred_element_type=F32
@@ -509,7 +642,9 @@
         head_out.reshape(row_count, HD), attn_panel[:, 3 * HD :],
         (((1,), (1,)), ((), ())), preferred_element_type=F32,
     ).astype(BF)
-    stream, stream_full = call_reduce_and_gather(partial_value, cell_rows)
+    stream, stream_full, up_panel, down_panel = call_reduce_and_gather(
+        partial_value, cell_rows, shares
+    )
     normed_ffn = rms_scale(stream_full.astype(F32), ffn_gain).astype(BF)
     hidden = jax.nn.gelu(
         jnp.dot(normed_ffn, up_panel, preferred_element_type=F32), approximate=False

time: 199 us -> 190 us (0.955)
  Pallas kernels: 168 us -> 156 us
  starting transfers between devices: 5.56 us -> 8.96 us
    pallas_call x1, Pallas kernels: 99.1 us -> 82.1 us  [gather_all(): pl.pallas_call(panels_and_cells, name='panels_and_cells', out_shape=[jax....]
    ppermute x1, starting transfers between devices: 2.06 us -> 6.41 us  [extended(): after = lax.ppermute(shard[:width], axis, down)]
    pallas_call x1, Pallas kernels: 42.6 us -> 46.9 us  [call_reduce_and_gather(): pl.pallas_call(reduce_and_gather, name='reduce_and_gather', out_shape=[ja...]
where the time goes in v4:
time: 190 us; the launch traced here: 189 us
  Pallas kernels  156 us (82%)
  matrix products  14.7 us (8%)
  starting transfers between devices  8.96 us (5%)
  other arithmetic  4.7 us (2%)
  local copies, waits for them, and re-layouts  2.88 us (2%)
    pallas_call x1, Pallas kernels, gather_all(): pl.pallas_call(panels_and_cells, name='panels_and_cells', out_shape=[jax....  82.1 us
    pallas_call x1, Pallas kernels, call_reduce_and_gather(): pl.pallas_call(reduce_and_gather, name='reduce_and_gather', out_shape=[ja...  46.9 us
    pallas_call x1, Pallas kernels, call_reduce_only(): pl.pallas_call(reduce_only, name='reduce_only', out_shape=jax.ShapeDtypeS...  27 us
    dot_general x1, matrix products, on_device(): lax.dot_general(hidden, down_panel, (((1,), (1,)), ((), ())), preferred_e...  8.1 us
    ppermute x1, starting transfers between devices, extended(): after = lax.ppermute(shard[:width], axis, down)  6.41 us
    reduce_sum x2, other arithmetic, rms_scale(): mean_square = jnp.mean(values * values, axis=-1, keepdims=True)  4.45 us
  transfers between devices with their start and end apart: 2, of which 2 were waited for; matrix products, arithmetic and copies ran while one was open for 0% of the time, Pallas kernels for 0%

profile of v4, /device:TPU:1, one launch (start us, length us, event | category | flops | bytes accessed | tf_op | source)
XLA Modules:
  0.0 188.8 jit_solution(9774676410282909144)
XLA Ops:
  0.0 0.0 copy-start.4
  0.0 82.1 %panels_and_cells.1 = (bf16[512,2048]{1,0:T(8,128)(2,1)}, bf16[16,2,2,32,512]{4,3,2,1,0:T(8,128)(2,1)}, bf16[4,32,512]{2,1,0:T(8,128)(2,1)}) custom-call(bf16[512,256]{1,0:T(8,128)(2,1)} %cell.3, bf16[16,2,2,32,512]{4,3,2,1,0:T(8,128)(2,1)} %bitcast.28, s32[64]{0:T(128)} %slot.1), custom_call_target="tpu_custom_call" | custom-call | tf_op jit(solution)/shard_map/panels_and_cells/pallas_call | solution.py:323
  82.1 0.0 copy-start.1
  82.1 2.2 %fusion = f32[512]{0:T(512)S(1)} fusion(bf16[512,2048]{1,0:T(8,128)(2,1)} %get-tuple-element.12), kind=kLoop, calls=%fused_computation.4 | loop fusion | flops 3145216 | bytes 2099200 | tf_op jit(solution)/shard_map/reduce_sum | solution.py:606
  84.4 0.0 copy-done.4
  84.4 0.0 copy-done.1
  84.4 0.0 copy-start.3
  84.4 2.7 %fusion.17 = bf16[512,384]{1,0:T(8,128)(2,1)S(1)} fusion(bf16[2048,512]{1,0:T(8,128)(2,1)} %bitcast.31, bf16[512,2048]{1,0:T(8,128)(2,1)S(1)} %copy-done.1, f32[2048]{0:T(1024)S(1)} %copy-done.4, f32[512]{0:T(512)S(1)} %add_rsqrt_fusion.1), kind=kOutput, calls=%fused_computation.24 | convolution fusion | flops 809697280 | bytes 4073472 | tf_op jit(solution)/shard_map/dot_general | solution.py:620
  87.1 0.0 copy-start.2
  87.2 6.4 %collective-permute-start.1 = (bf16[256,256]{1,0:T(8,128)(2,1)S(1)}, bf16[256,256]{1,0:T(8,128)(2,1)S(1)}, u32[]{:S(2)}, u32[]{:S(2)}) collective-permute-start(bf16[256,256]{1,0:T(8,128)(2,1)S(1)} %get-tuple-element.21), channel_id=1, source_target_pairs={{8,0},{16,8},{24,16},{32,24},{40,32},{48,40},{56,48},{64,56},{72,6... | collective-permute-start | bytes 393224 | tf_op jit(solution)/shard_map/ppermute | solution.py:601
  93.6 2.5 %collective-permute-start = (bf16[256,256]{1,0:T(8,128)(2,1)S(1)}, bf16[256,256]{1,0:T(8,128)(2,1)S(1)}, u32[]{:S(2)}, u32[]{:S(2)}) collective-permute-start(bf16[256,256]{1,0:T(8,128)(2,1)S(1)} %get-tuple-element.22), channel_id=1, source_target_pairs={{0,8},{8,16},{16,24},{24,32},{32,40},{40,48},{48,56},{56,64},{64,7... | collective-permute-start | bytes 393224 | tf_op jit(solution)/shard_map/ppermute | solution.py:600
  96.1 0.1 add_add_fusion
  96.2 0.0 copy-done.3
  96.2 0.1 copy.13
  96.3 0.1 stack.20
  96.4 0.1 compare_reduce_fusion
  96.5 0.2 collective-permute-done.1
  96.7 1.2 collective-permute-done
  97.9 0.1 pad_maximum_fusion
  97.9 0.1 stack.22
  98.0 0.1 stack.21
  98.1 0.0 copy-done.2
  98.1 0.0 slice-start
  98.1 0.1 stack.18
  98.2 0.1 stack.19
  98.3 0.1 copy_dynamic-update-slice_fusion.3
  98.4 0.1 copy_dynamic-update-slice_fusion.2
  98.5 0.1 copy_dynamic-update-slice_fusion.1
  98.5 0.1 copy_dynamic-update-slice_fusion
  98.6 0.4 slice-done
  99.0 0.4 fusion.102
  99.4 0.4 fusion.22
  99.8 3.1 %convolution_convert_fusion.part = bf16[512,2048]{1,0:T(8,128)(2,1)} fusion(bf16[512,128]{1,0:T(8,128)(2,1)S(1)} %bitcast.33, bf16[2048,512]{1,0:T(8,128)(2,1)} %bitcast.32), kind=kOutput, calls=%fused_computation.10 | convolution fusion | flops 269484032 | bytes 2752512 | tf_op jit(solution)/shard_map/dot_general | solution.py:641
  102.9 0.0 copy-start.5
  102.9 46.9 %reduce_and_gather.1 = (bf16[512,256]{1,0:T(8,128)(2,1)}, bf16[512,2048]{1,0:T(8,128)(2,1)}, bf16[16,2,1,64,512]{4,3,2,1,0:T(8,128)(2,1)}, bf16[16,2,1,64,512]{4,3,2,1,0:T(8,128)(2,1)}) custom-call(bf16[512,2048]{1,0:T(8,128)(2,1)} %convolution_convert_fusion.part, bf16[512,256]{1,0:T(8,128)(2,1)} %cell.3, bf16[2,64,512]{2,1,0:T(8,128)(2,1)} %bitcast.30), custom_call_target="tpu_custom_call" | custom-call | tf_op jit(solution)/shard_map/reduce_and_gather/pallas_call | solution.py:562
  149.8 0.0 copy-start
  149.8 2.2 %fusion.3 = f32[512]{0:T(512)S(1)} fusion(bf16[512,2048]{1,0:T(8,128)(2,1)} %get-tuple-element.15), kind=kLoop, calls=%fused_computation.7 | loop fusion | flops 3145216 | bytes 2099200 | tf_op jit(solution)/shard_map/reduce_sum | solution.py:606
  152.1 0.0 copy-done.5
  152.1 0.0 copy-done
  152.1 8.1 %convolution_convert_fusion.1.part = bf16[512,2048]{1,0:T(8,128)(2,1)} fusion(bf16[2048,512]{1,0:T(8,128)(2,1)} %bitcast.35, bf16[2048,512]{1,0:T(8,128)(2,1)} %bitcast.34, bf16[512,2048]{1,0:T(8,128)(2,1)S(1)} %copy-done, f32[2048]{0:T(1024)S(1)} %copy-done.5, f32[512]{0:T(512)S(1)} %add_rsqrt_fusion), kind=kOutput, calls=%fused_computation.11 | convolution fusion | flops 2169765888 | bytes 8398848 | tf_op jit(solution)/shard_map/dot_general | solution.py:652
  160.2 27.0 %reduce_only.1 = bf16[512,256]{1,0:T(8,128)(2,1)} custom-call(bf16[512,2048]{1,0:T(8,128)(2,1)} %convolution_convert_fusion.1.part, bf16[512,256]{1,0:T(8,128)(2,1)} %get-tuple-element.18.base), custom_call_target="tpu_custom_call" | custom-call | tf_op jit(solution)/shard_map/reduce_only/pallas_call | solution.py:583
  187.2 1.7 copy.33
  (6 shorter events, 0.1 us)
Async XLA Ops:
  0.0 84.4 %copy-start.4 = (f32[2048]{0:T(1024)S(1)}, f32[2048]{0:T(1024)}, u32[]{:S(2)}) copy-start(f32[2048]{0:T(1024)} %param.7) | copy-start | bytes 24580
  82.1 2.3 %copy-start.1 = (bf16[512,2048]{1,0:T(8,128)(2,1)S(1)}, bf16[512,2048]{1,0:T(8,128)(2,1)}, u32[]{:S(2)}) copy-start(bf16[512,2048]{1,0:T(8,128)(2,1)} %get-tuple-element.12) | copy-start | bytes 6291460
  84.4 11.9 %copy-start.3 = (s32[4,3]{1,0:T(4,128)S(1)}, s32[4,3]{1,0:T(4,128)}, u32[]{:S(2)}) copy-start(s32[4,3]{1,0:T(4,128)} %param.11) | copy-start | bytes 148
  87.1 11.0 %copy-start.2 = (bf16[512,384]{1,0:T(8,128)(2,1)}, bf16[512,384]{1,0:T(8,128)(2,1)S(1)}, u32[]{:S(2)}) copy-start(bf16[512,384]{1,0:T(8,128)(2,1)S(1)} %fusion.17) | copy-start | bytes 1179652
  87.2 9.5 %collective-permute-start.1 = (bf16[256,256]{1,0:T(8,128)(2,1)S(1)}, bf16[256,256]{1,0:T(8,128)(2,1)S(1)}, u32[]{:S(2)}, u32[]{:S(2)}) collective-permute-start(bf16[256,256]{1,0:T(8,128)(2,1)S(1)} %get-tuple-element.21), channel_id=1, source_target_pairs={{8,0},{16,8},{24,16},{32,24},{40,32},{48,40},{56,48},{64,56},{72,6... | collective-permute-start | bytes 393224 | tf_op jit(solution)/shard_map/ppermute | solution.py:601
  93.6 4.3 %collective-permute-start = (bf16[256,256]{1,0:T(8,128)(2,1)S(1)}, bf16[256,256]{1,0:T(8,128)(2,1)S(1)}, u32[]{:S(2)}, u32[]{:S(2)}) collective-permute-start(bf16[256,256]{1,0:T(8,128)(2,1)S(1)} %get-tuple-element.22), channel_id=1, source_target_pairs={{0,8},{8,16},{16,24},{24,32},{32,40},{40,48},{48,56},{56,64},{64,7... | collective-permute-start | bytes 393224 | tf_op jit(solution)/shard_map/ppermute | solution.py:600
  98.1 0.9 slice-start
  102.9 49.2 %copy-start.5 = (f32[2048]{0:T(1024)S(1)}, f32[2048]{0:T(1024)}, u32[]{:S(2)}) copy-start(f32[2048]{0:T(1024)} %param.8) | copy-start | bytes 24580
  149.8 2.3 %copy-start = (bf16[512,2048]{1,0:T(8,128)(2,1)S(1)}, bf16[512,2048]{1,0:T(8,128)(2,1)}, u32[]{:S(2)}) copy-start(bf16[512,2048]{1,0:T(8,128)(2,1)} %get-tuple-element.15) | copy-start | bytes 6291460

commit v5 on v4

--- a/solution.py
+++ b/solution.py
@@ -268,16 +268,16 @@
     columns = gath.at[:, pl.ds(pl.multiple_of(n * 256, 256), 256)]
     own = pltpu.make_async_copy(cell, columns, own_sem)
     own.start()
+    first = range(2 * PARTS)
+    later = range(2 * PARTS, 3 * PARTS)
+    pick.to_partner().wait_recv()
+    for i in first:
+        pick.begin(i)
     sends = []
     for k in range(1, NN):
         copy = remote(cell, columns, nsend.at[k - 1], nrecv.at[k - 1], w, peers[k - 1])
         copy.start()
         sends.append(copy)
-    first = range(2 * PARTS)
-    later = range(2 * PARTS, 3 * PARTS)
-    pick.to_partner().wait_recv()
-    for i in first:
-        pick.begin(i)
 
     def both(s):
         for i in first:
@@ -350,7 +350,8 @@
         self.devices = [self.right, self.left, self.pair]
 
 
-CH = 4
+CH = 8
+HALF = CH // 2
 ROWS = 512 // CH
 
 
@@ -510,12 +511,12 @@
         kept.append(copy)
     for c in range(CH):
         add.forward(c)
-        if c % 2 == 1:
-            fan.relay(c // 2 + 1)
+        if c % HALF == HALF - 1:
+            fan.relay(c // HALF + 1)
     for c in range(CH):
         add.cross(c)
-        if c % 2 == 1:
-            fan.relay(c // 2 + 3)
+        if c % HALF == HALF - 1:
+            fan.relay(c // HALF + 3)
     columns = gath.at[:, pl.ds(pl.multiple_of(net.n * 256, 256), 256)]
     for c in range(CH):
         total = cell[rows_of(c)].astype(F32) + add.total(c)

time: 190 us -> 195 us (1.026)
  Pallas kernels: 156 us -> 161 us
    pallas_call x1, Pallas kernels: 82.1 us -> 85.7 us  [gather_all(): pl.pallas_call(panels_and_cells, name='panels_and_cells', out_shape=[jax....]
where the time goes in v5:
time: 195 us; the launch traced here: 194 us
  Pallas kernels  161 us (83%)
  matrix products  14.7 us (8%)
  starting transfers between devices  9 us (5%)
  other arithmetic  4.7 us (2%)
  local copies, waits for them, and re-layouts  2.88 us (1%)
    pallas_call x1, Pallas kernels, gather_all(): pl.pallas_call(panels_and_cells, name='panels_and_cells', out_shape=[jax....  85.7 us
    pallas_call x1, Pallas kernels, call_reduce_and_gather(): pl.pallas_call(reduce_and_gather, name='reduce_and_gather', out_shape=[ja...  47 us
    pallas_call x1, Pallas kernels, call_reduce_only(): pl.pallas_call(reduce_only, name='reduce_only', out_shape=jax.ShapeDtypeS...  28.5 us
    dot_general x1, matrix products, on_device(): lax.dot_general(hidden, down_panel, (((1,), (1,)), ((), ())), preferred_e...  8.1 us
    ppermute x1, starting transfers between devices, extended(): after = lax.ppermute(shard[:width], axis, down)  6.42 us
    reduce_sum x2, other arithmetic, rms_scale(): mean_square = jnp.mean(values * values, axis=-1, keepdims=True)  4.45 us
  transfers between devices with their start and end apart: 2, of which 2 were waited for; matrix products, arithmetic and copies ran while one was open for 0% of the time, Pallas kernels for 0%

profile of v5, /device:TPU:1, one launch (start us, length us, event | category | flops | bytes accessed | tf_op | source)
XLA Modules:
  0.0 194.1 jit_solution(9211917929255096702)
XLA Ops:
  0.0 0.0 copy-start.4
  0.0 85.7 %panels_and_cells.1 = (bf16[512,2048]{1,0:T(8,128)(2,1)}, bf16[16,2,2,32,512]{4,3,2,1,0:T(8,128)(2,1)}, bf16[4,32,512]{2,1,0:T(8,128)(2,1)}) custom-call(bf16[512,256]{1,0:T(8,128)(2,1)} %cell.3, bf16[16,2,2,32,512]{4,3,2,1,0:T(8,128)(2,1)} %bitcast.28, s32[64]{0:T(128)} %slot.1), custom_call_target="tpu_custom_call" | custom-call | tf_op jit(solution)/shard_map/panels_and_cells/pallas_call | solution.py:323
  85.7 0.0 copy-start.1
  85.7 2.2 %fusion = f32[512]{0:T(512)S(1)} fusion(bf16[512,2048]{1,0:T(8,128)(2,1)} %get-tuple-element.12), kind=kLoop, calls=%fused_computation.4 | loop fusion | flops 3145216 | bytes 2099200 | tf_op jit(solution)/shard_map/reduce_sum | solution.py:607
  87.9 0.0 copy-done.4
  87.9 0.0 copy-done.1
  88.0 0.0 copy-start.3
  88.0 2.7 %fusion.17 = bf16[512,384]{1,0:T(8,128)(2,1)S(1)} fusion(bf16[2048,512]{1,0:T(8,128)(2,1)} %bitcast.31, bf16[512,2048]{1,0:T(8,128)(2,1)S(1)} %copy-done.1, f32[2048]{0:T(1024)S(1)} %copy-done.4, f32[512]{0:T(512)S(1)} %add_rsqrt_fusion.1), kind=kOutput, calls=%fused_computation.24 | convolution fusion | flops 809697280 | bytes 4073472 | tf_op jit(solution)/shard_map/dot_general | solution.py:621
  90.7 0.0 copy-start.2
  90.7 6.4 %collective-permute-start.1 = (bf16[256,256]{1,0:T(8,128)(2,1)S(1)}, bf16[256,256]{1,0:T(8,128)(2,1)S(1)}, u32[]{:S(2)}, u32[]{:S(2)}) collective-permute-start(bf16[256,256]{1,0:T(8,128)(2,1)S(1)} %get-tuple-element.21), channel_id=1, source_target_pairs={{8,0},{16,8},{24,16},{32,24},{40,32},{48,40},{56,48},{64,56},{72,6... | collective-permute-start | bytes 393224 | tf_op jit(solution)/shard_map/ppermute | solution.py:602
  97.2 2.6 %collective-permute-start = (bf16[256,256]{1,0:T(8,128)(2,1)S(1)}, bf16[256,256]{1,0:T(8,128)(2,1)S(1)}, u32[]{:S(2)}, u32[]{:S(2)}) collective-permute-start(bf16[256,256]{1,0:T(8,128)(2,1)S(1)} %get-tuple-element.22), channel_id=1, source_target_pairs={{0,8},{8,16},{16,24},{24,32},{32,40},{40,48},{48,56},{56,64},{64,7... | collective-permute-start | bytes 393224 | tf_op jit(solution)/shard_map/ppermute | solution.py:601
  99.8 0.1 add_add_fusion
  99.9 0.0 copy-done.3
  99.9 0.1 copy.13
  100.0 0.1 stack.20
  100.0 0.1 compare_reduce_fusion
  100.1 0.2 collective-permute-done.1
  100.3 1.2 collective-permute-done
  101.5 0.1 pad_maximum_fusion
  101.6 0.1 stack.22
  101.6 0.1 stack.21
  101.7 0.0 copy-done.2
  101.7 0.0 slice-start
  101.7 0.1 stack.18
  101.8 0.1 stack.19
  101.9 0.1 copy_dynamic-update-slice_fusion.3
  102.0 0.1 copy_dynamic-update-slice_fusion.2
  102.1 0.1 copy_dynamic-update-slice_fusion.1
  102.2 0.1 copy_dynamic-update-slice_fusion
  102.2 0.4 slice-done
  102.6 0.4 fusion.102
  103.0 0.4 fusion.22
  103.5 3.1 %convolution_convert_fusion.part = bf16[512,2048]{1,0:T(8,128)(2,1)} fusion(bf16[512,128]{1,0:T(8,128)(2,1)S(1)} %bitcast.33, bf16[2048,512]{1,0:T(8,128)(2,1)} %bitcast.32), kind=kOutput, calls=%fused_computation.10 | convolution fusion | flops 269484032 | bytes 2752512 | tf_op jit(solution)/shard_map/dot_general | solution.py:642
  106.5 0.0 copy-start.5
  106.5 47.0 %reduce_and_gather.1 = (bf16[512,256]{1,0:T(8,128)(2,1)}, bf16[512,2048]{1,0:T(8,128)(2,1)}, bf16[16,2,1,64,512]{4,3,2,1,0:T(8,128)(2,1)}, bf16[16,2,1,64,512]{4,3,2,1,0:T(8,128)(2,1)}) custom-call(bf16[512,2048]{1,0:T(8,128)(2,1)} %convolution_convert_fusion.part, bf16[512,256]{1,0:T(8,128)(2,1)} %cell.3, bf16[2,64,512]{2,1,0:T(8,128)(2,1)} %bitcast.30), custom_call_target="tpu_custom_call" | custom-call | tf_op jit(solution)/shard_map/reduce_and_gather/pallas_call | solution.py:563
  153.5 0.0 copy-start
  153.5 2.2 %fusion.3 = f32[512]{0:T(512)S(1)} fusion(bf16[512,2048]{1,0:T(8,128)(2,1)} %get-tuple-element.15), kind=kLoop, calls=%fused_computation.7 | loop fusion | flops 3145216 | bytes 2099200 | tf_op jit(solution)/shard_map/reduce_sum | solution.py:607
  155.8 0.0 copy-done.5
  155.8 0.0 copy-done
  155.8 8.1 %convolution_convert_fusion.1.part = bf16[512,2048]{1,0:T(8,128)(2,1)} fusion(bf16[2048,512]{1,0:T(8,128)(2,1)} %bitcast.35, bf16[2048,512]{1,0:T(8,128)(2,1)} %bitcast.34, bf16[512,2048]{1,0:T(8,128)(2,1)S(1)} %copy-done, f32[2048]{0:T(1024)S(1)} %copy-done.5, f32[512]{0:T(512)S(1)} %add_rsqrt_fusion), kind=kOutput, calls=%fused_computation.11 | convolution fusion | flops 2169765888 | bytes 8398848 | tf_op jit(solution)/shard_map/dot_general | solution.py:653
  163.9 28.5 %reduce_only.1 = bf16[512,256]{1,0:T(8,128)(2,1)} custom-call(bf16[512,2048]{1,0:T(8,128)(2,1)} %convolution_convert_fusion.1.part, bf16[512,256]{1,0:T(8,128)(2,1)} %get-tuple-element.18.base), custom_call_target="tpu_custom_call" | custom-call | tf_op jit(solution)/shard_map/reduce_only/pallas_call | solution.py:584
  192.4 1.7 copy.33
  (6 shorter events, 0.1 us)
Async XLA Ops:
  0.0 87.9 %copy-start.4 = (f32[2048]{0:T(1024)S(1)}, f32[2048]{0:T(1024)}, u32[]{:S(2)}) copy-start(f32[2048]{0:T(1024)} %param.7) | copy-start | bytes 24580
  85.7 2.3 %copy-start.1 = (bf16[512,2048]{1,0:T(8,128)(2,1)S(1)}, bf16[512,2048]{1,0:T(8,128)(2,1)}, u32[]{:S(2)}) copy-start(bf16[512,2048]{1,0:T(8,128)(2,1)} %get-tuple-element.12) | copy-start | bytes 6291460
  88.0 11.9 %copy-start.3 = (s32[4,3]{1,0:T(4,128)S(1)}, s32[4,3]{1,0:T(4,128)}, u32[]{:S(2)}) copy-start(s32[4,3]{1,0:T(4,128)} %param.11) | copy-start | bytes 148
  90.7 11.0 %copy-start.2 = (bf16[512,384]{1,0:T(8,128)(2,1)}, bf16[512,384]{1,0:T(8,128)(2,1)S(1)}, u32[]{:S(2)}) copy-start(bf16[512,384]{1,0:T(8,128)(2,1)S(1)} %fusion.17) | copy-start | bytes 1179652
  90.7 9.5 %collective-permute-start.1 = (bf16[256,256]{1,0:T(8,128)(2,1)S(1)}, bf16[256,256]{1,0:T(8,128)(2,1)S(1)}, u32[]{:S(2)}, u32[]{:S(2)}) collective-permute-start(bf16[256,256]{1,0:T(8,128)(2,1)S(1)} %get-tuple-element.21), channel_id=1, source_target_pairs={{8,0},{16,8},{24,16},{32,24},{40,32},{48,40},{56,48},{64,56},{72,6... | collective-permute-start | bytes 393224 | tf_op jit(solution)/shard_map/ppermute | solution.py:602
  97.2 4.3 %collective-permute-start = (bf16[256,256]{1,0:T(8,128)(2,1)S(1)}, bf16[256,256]{1,0:T(8,128)(2,1)S(1)}, u32[]{:S(2)}, u32[]{:S(2)}) collective-permute-start(bf16[256,256]{1,0:T(8,128)(2,1)S(1)} %get-tuple-element.22), channel_id=1, source_target_pairs={{0,8},{8,16},{16,24},{24,32},{32,40},{40,48},{48,56},{56,64},{64,7... | collective-permute-start | bytes 393224 | tf_op jit(solution)/shard_map/ppermute | solution.py:601
  101.7 0.9 slice-start
  106.5 49.2 %copy-start.5 = (f32[2048]{0:T(1024)S(1)}, f32[2048]{0:T(1024)}, u32[]{:S(2)}) copy-start(f32[2048]{0:T(1024)} %param.8) | copy-start | bytes 24580
  153.5 2.3 %copy-start = (bf16[512,2048]{1,0:T(8,128)(2,1)S(1)}, bf16[512,2048]{1,0:T(8,128)(2,1)}, u32[]{:S(2)}) copy-start(bf16[512,2048]{1,0:T(8,128)(2,1)} %get-tuple-element.15) | copy-start | bytes 6291460

commit v6 on v5

--- a/solution.py
+++ b/solution.py
@@ -350,7 +350,7 @@
         self.devices = [self.right, self.left, self.pair]
 
 
-CH = 8
+CH = 4
 HALF = CH // 2
 ROWS = 512 // CH
 

time: 195 us -> 195 us (level)
    pallas_call x1, Pallas kernels: 28.5 us -> 26.3 us  [call_reduce_only(): pl.pallas_call(reduce_only, name='reduce_only', out_shape=jax.ShapeDtypeS...]
where the time goes in v6:
time: 195 us; the launch traced here: 193 us
  Pallas kernels  160 us (82%)
  matrix products  14.7 us (8%)
  starting transfers between devices  9 us (5%)
  other arithmetic  4.7 us (2%)
  local copies, waits for them, and re-layouts  2.88 us (1%)
    pallas_call x1, Pallas kernels, gather_all(): pl.pallas_call(panels_and_cells, name='panels_and_cells', out_shape=[jax....  85.7 us
    pallas_call x1, Pallas kernels, call_reduce_and_gather(): pl.pallas_call(reduce_and_gather, name='reduce_and_gather', out_shape=[ja...  47.7 us
    pallas_call x1, Pallas kernels, call_reduce_only(): pl.pallas_call(reduce_only, name='reduce_only', out_shape=jax.ShapeDtypeS...  26.3 us
    dot_general x1, matrix products, on_device(): lax.dot_general(hidden, down_panel, (((1,), (1,)), ((), ())), preferred_e...  8.1 us
    ppermute x1, starting transfers between devices, extended(): after = lax.ppermute(shard[:width], axis, down)  6.42 us
    reduce_sum x2, other arithmetic, rms_scale(): mean_square = jnp.mean(values * values, axis=-1, keepdims=True)  4.45 us
  transfers between devices with their start and end apart: 2, of which 2 were waited for; matrix products, arithmetic and copies ran while one was open for 0% of the time, Pallas kernels for 0%

profile of v6, /device:TPU:1, one launch (start us, length us, event | category | flops | bytes accessed | tf_op | source)
XLA Modules:
  0.0 192.5 jit_solution(7760127184304654451)
XLA Ops:
  0.0 0.0 copy-start.4
  0.0 85.7 %panels_and_cells.1 = (bf16[512,2048]{1,0:T(8,128)(2,1)}, bf16[16,2,2,32,512]{4,3,2,1,0:T(8,128)(2,1)}, bf16[4,32,512]{2,1,0:T(8,128)(2,1)}) custom-call(bf16[512,256]{1,0:T(8,128)(2,1)} %cell.3, bf16[16,2,2,32,512]{4,3,2,1,0:T(8,128)(2,1)} %bitcast.28, s32[64]{0:T(128)} %slot.1), custom_call_target="tpu_custom_call" | custom-call | tf_op jit(solution)/shard_map/panels_and_cells/pallas_call | solution.py:323
  85.7 0.0 copy-start.1
  85.7 2.2 %fusion = f32[512]{0:T(512)S(1)} fusion(bf16[512,2048]{1,0:T(8,128)(2,1)} %get-tuple-element.12), kind=kLoop, calls=%fused_computation.4 | loop fusion | flops 3145216 | bytes 2099200 | tf_op jit(solution)/shard_map/reduce_sum | solution.py:607
  87.9 0.0 copy-done.4
  87.9 0.0 copy-done.1
  88.0 0.0 copy-start.3
  88.0 2.7 %fusion.17 = bf16[512,384]{1,0:T(8,128)(2,1)S(1)} fusion(bf16[2048,512]{1,0:T(8,128)(2,1)} %bitcast.31, bf16[512,2048]{1,0:T(8,128)(2,1)S(1)} %copy-done.1, f32[2048]{0:T(1024)S(1)} %copy-done.4, f32[512]{0:T(512)S(1)} %add_rsqrt_fusion.1), kind=kOutput, calls=%fused_computation.24 | convolution fusion | flops 809697280 | bytes 4073472 | tf_op jit(solution)/shard_map/dot_general | solution.py:621
  90.7 0.0 copy-start.2
  90.7 6.4 %collective-permute-start.1 = (bf16[256,256]{1,0:T(8,128)(2,1)S(1)}, bf16[256,256]{1,0:T(8,128)(2,1)S(1)}, u32[]{:S(2)}, u32[]{:S(2)}) collective-permute-start(bf16[256,256]{1,0:T(8,128)(2,1)S(1)} %get-tuple-element.21), channel_id=1, source_target_pairs={{8,0},{16,8},{24,16},{32,24},{40,32},{48,40},{56,48},{64,56},{72,6... | collective-permute-start | bytes 393224 | tf_op jit(solution)/shard_map/ppermute | solution.py:602
  97.2 2.6 %collective-permute-start = (bf16[256,256]{1,0:T(8,128)(2,1)S(1)}, bf16[256,256]{1,0:T(8,128)(2,1)S(1)}, u32[]{:S(2)}, u32[]{:S(2)}) collective-permute-start(bf16[256,256]{1,0:T(8,128)(2,1)S(1)} %get-tuple-element.22), channel_id=1, source_target_pairs={{0,8},{8,16},{16,24},{24,32},{32,40},{40,48},{48,56},{56,64},{64,7... | collective-permute-start | bytes 393224 | tf_op jit(solution)/shard_map/ppermute | solution.py:601
  99.8 0.1 add_add_fusion
  99.9 0.0 copy-done.3
  99.9 0.1 copy.13
  100.0 0.1 stack.20
  100.0 0.1 compare_reduce_fusion
  100.1 0.2 collective-permute-done.1
  100.3 1.2 collective-permute-done
  101.5 0.1 pad_maximum_fusion
  101.6 0.1 stack.22
  101.6 0.1 stack.21
  101.7 0.0 copy-done.2
  101.7 0.0 slice-start
  101.7 0.1 stack.18
  101.8 0.1 stack.19
  101.9 0.1 copy_dynamic-update-slice_fusion.3
  102.0 0.1 copy_dynamic-update-slice_fusion.2
  102.1 0.1 copy_dynamic-update-slice_fusion.1
  102.2 0.1 copy_dynamic-update-slice_fusion
  102.2 0.4 slice-done
  102.6 0.4 fusion.102
  103.0 0.4 fusion.22
  103.5 3.1 %convolution_convert_fusion.part = bf16[512,2048]{1,0:T(8,128)(2,1)} fusion(bf16[512,128]{1,0:T(8,128)(2,1)S(1)} %bitcast.33, bf16[2048,512]{1,0:T(8,128)(2,1)} %bitcast.32), kind=kOutput, calls=%fused_computation.10 | convolution fusion | flops 269484032 | bytes 2752512 | tf_op jit(solution)/shard_map/dot_general | solution.py:642
  106.5 0.0 copy-start.5
  106.5 47.7 %reduce_and_gather.1 = (bf16[512,256]{1,0:T(8,128)(2,1)}, bf16[512,2048]{1,0:T(8,128)(2,1)}, bf16[16,2,1,64,512]{4,3,2,1,0:T(8,128)(2,1)}, bf16[16,2,1,64,512]{4,3,2,1,0:T(8,128)(2,1)}) custom-call(bf16[512,2048]{1,0:T(8,128)(2,1)} %convolution_convert_fusion.part, bf16[512,256]{1,0:T(8,128)(2,1)} %cell.3, bf16[2,64,512]{2,1,0:T(8,128)(2,1)} %bitcast.30), custom_call_target="tpu_custom_call" | custom-call | tf_op jit(solution)/shard_map/reduce_and_gather/pallas_call | solution.py:563
  154.2 0.0 copy-start
  154.2 2.2 %fusion.3 = f32[512]{0:T(512)S(1)} fusion(bf16[512,2048]{1,0:T(8,128)(2,1)} %get-tuple-element.15), kind=kLoop, calls=%fused_computation.7 | loop fusion | flops 3145216 | bytes 2099200 | tf_op jit(solution)/shard_map/reduce_sum | solution.py:607
  156.5 0.0 copy-done.5
  156.5 0.0 copy-done
  156.5 8.1 %convolution_convert_fusion.1.part = bf16[512,2048]{1,0:T(8,128)(2,1)} fusion(bf16[2048,512]{1,0:T(8,128)(2,1)} %bitcast.35, bf16[2048,512]{1,0:T(8,128)(2,1)} %bitcast.34, bf16[512,2048]{1,0:T(8,128)(2,1)S(1)} %copy-done, f32[2048]{0:T(1024)S(1)} %copy-done.5, f32[512]{0:T(512)S(1)} %add_rsqrt_fusion), kind=kOutput, calls=%fused_computation.11 | convolution fusion | flops 2169765888 | bytes 8398848 | tf_op jit(solution)/shard_map/dot_general | solution.py:653
  164.6 26.3 %reduce_only.1 = bf16[512,256]{1,0:T(8,128)(2,1)} custom-call(bf16[512,2048]{1,0:T(8,128)(2,1)} %convolution_convert_fusion.1.part, bf16[512,256]{1,0:T(8,128)(2,1)} %get-tuple-element.18.base), custom_call_target="tpu_custom_call" | custom-call | tf_op jit(solution)/shard_map/reduce_only/pallas_call | solution.py:584
  190.9 1.7 copy.33
  (6 shorter events, 0.1 us)
Async XLA Ops:
  0.0 87.9 %copy-start.4 = (f32[2048]{0:T(1024)S(1)}, f32[2048]{0:T(1024)}, u32[]{:S(2)}) copy-start(f32[2048]{0:T(1024)} %param.7) | copy-start | bytes 24580
  85.7 2.3 %copy-start.1 = (bf16[512,2048]{1,0:T(8,128)(2,1)S(1)}, bf16[512,2048]{1,0:T(8,128)(2,1)}, u32[]{:S(2)}) copy-start(bf16[512,2048]{1,0:T(8,128)(2,1)} %get-tuple-element.12) | copy-start | bytes 6291460
  88.0 11.9 %copy-start.3 = (s32[4,3]{1,0:T(4,128)S(1)}, s32[4,3]{1,0:T(4,128)}, u32[]{:S(2)}) copy-start(s32[4,3]{1,0:T(4,128)} %param.11) | copy-start | bytes 148
  90.7 11.0 %copy-start.2 = (bf16[512,384]{1,0:T(8,128)(2,1)}, bf16[512,384]{1,0:T(8,128)(2,1)S(1)}, u32[]{:S(2)}) copy-start(bf16[512,384]{1,0:T(8,128)(2,1)S(1)} %fusion.17) | copy-start | bytes 1179652
  90.7 9.5 %collective-permute-start.1 = (bf16[256,256]{1,0:T(8,128)(2,1)S(1)}, bf16[256,256]{1,0:T(8,128)(2,1)S(1)}, u32[]{:S(2)}, u32[]{:S(2)}) collective-permute-start(bf16[256,256]{1,0:T(8,128)(2,1)S(1)} %get-tuple-element.21), channel_id=1, source_target_pairs={{8,0},{16,8},{24,16},{32,24},{40,32},{48,40},{56,48},{64,56},{72,6... | collective-permute-start | bytes 393224 | tf_op jit(solution)/shard_map/ppermute | solution.py:602
  97.2 4.3 %collective-permute-start = (bf16[256,256]{1,0:T(8,128)(2,1)S(1)}, bf16[256,256]{1,0:T(8,128)(2,1)S(1)}, u32[]{:S(2)}, u32[]{:S(2)}) collective-permute-start(bf16[256,256]{1,0:T(8,128)(2,1)S(1)} %get-tuple-element.22), channel_id=1, source_target_pairs={{0,8},{8,16},{16,24},{24,32},{32,40},{40,48},{48,56},{56,64},{64,7... | collective-permute-start | bytes 393224 | tf_op jit(solution)/shard_map/ppermute | solution.py:601
  101.7 0.9 slice-start
  106.5 49.9 %copy-start.5 = (f32[2048]{0:T(1024)S(1)}, f32[2048]{0:T(1024)}, u32[]{:S(2)}) copy-start(f32[2048]{0:T(1024)} %param.8) | copy-start | bytes 24580
  154.2 2.3 %copy-start = (bf16[512,2048]{1,0:T(8,128)(2,1)S(1)}, bf16[512,2048]{1,0:T(8,128)(2,1)}, u32[]{:S(2)}) copy-start(bf16[512,2048]{1,0:T(8,128)(2,1)} %get-tuple-element.15) | copy-start | bytes 6291460
